TPU v7x, 256 devices: a whole 4x4x8 slice. The times are simulated.
256 devices in a mesh: tile: 32 (over y, z_hi, x), store: 8 (over z_lo, core).
Axes of the slice: x: 4, y: 4, z: 8 (z_hi: 2, z_lo: 4; z = z_hi * 4 + z_lo), core: 2. Of those that a mesh axis runs over, the one named last changes fastest.
Arguments:
- state: float32 [4, 64, 8, 4096], P(None, 'store', None, 'tile'), may hold values from -6 to 6
- cotangent: float32 [4, 64, 8, 4096], P(None, 'store', None, 'tile'), may hold values from -6 to 6
- land_mask: int32 [8, 4096], P(None, 'tile'), may hold values 0 or 1
- wet_count: int32 [8, 4096], P(None, 'tile'), may hold values from 1 to 64
- background: float32 [8, 4096], P(None, 'tile'), may hold values from 0.05 to 2
Outputs:
- state_grad: float32 [4, 64, 8, 4096], P(None, 'store', None, 'tile')
- background_grad: float32 [8, 4096], P(None, ('tile', 'store'))
All inputs are finite; a program needn't handle non-finite values. No bound on the sum of `land_mask` on one device may be relied on, other than what follows from the above.
Results may differ from a plain program's by a relative error of at most 0.00002.
Values sent between devices are 32-bit elements; how exact they have to be, the bound alone decides.
A program may use at most 64 MiB of HBM per device.

v0:
```python
import jax
import jax.numpy as jnp
from jax import lax
from jax.sharding import PartitionSpec as P

DIFFUSE = 0.1
ADVECT = 0.05
MIXING = 2.0
ALPHA_T = 0.6
BETA_S = 0.8


def padded(cells, sides, width):
    for axis, dim in sides:
        count = lax.axis_size(axis)
        head = lax.slice_in_dim(cells, 0, width, axis=dim)
        tail = lax.slice_in_dim(cells, cells.shape[dim] - width, cells.shape[dim], axis=dim)
        cells = jnp.concatenate(
            [
                lax.ppermute(tail, axis, [(i, (i + 1) % count) for i in range(count)]),
                cells,
                lax.ppermute(head, axis, [((i + 1) % count, i) for i in range(count)]),
            ],
            axis=dim,
        )
    return cells


def wet_of(land_mask, wet_count, level_ids):
    ocean = land_mask[None] == 1
    deep = level_ids[:, None, None] < wet_count[None]
    return jnp.logical_and(ocean, deep).astype(jnp.float32)


def hstep(state_pad, wet_pad):
    masked = state_pad * wet_pad
    middle = masked[..., 1:-1]
    wet_mid = wet_pad[..., 1:-1]
    eastern = masked[..., 2:]
    western = masked[..., :-2]
    wet_east = wet_pad[..., 2:]
    wet_west = wet_pad[..., :-2]
    rows_pad = ((0, 0), (0, 0), (1, 1), (0, 0))
    mid_rows = jnp.pad(middle, rows_pad)
    wet_rows = jnp.pad(wet_mid, rows_pad)
    northern = mid_rows[:, :, 2:]
    southern = mid_rows[:, :, :-2]
    wet_north = wet_rows[:, :, 2:]
    wet_south = wet_rows[:, :, :-2]
    lap = (
        wet_east * (eastern - middle)
        + wet_west * (western - middle)
        + wet_north * (northern - middle)
        + wet_south * (southern - middle)
    )
    inter = wet_mid * (middle + DIFFUSE * lap)
    zonal = middle[2]
    merid = middle[3]
    advect = (
        -ADVECT
        * wet_mid[0]
        * (zonal * (eastern[:2] - western[:2]) + merid * (northern[:2] - southern[:2]))
    )
    rows = state_pad.shape[2]
    latitude = 0.1 + 0.2 * (jnp.arange(rows, dtype=jnp.float32) + 0.5) / rows
    latitude = latitude[None, :, None]
    turn_u = latitude * merid
    turn_v = -latitude * zonal
    extra = jnp.concatenate([advect, turn_u[None], turn_v[None]], axis=0)
    return inter + extra


def solve_columns(upper_c, lower_c, diagonal, rhs):
    depth = rhs.shape[1]
    ratios = []
    values = []
    ratio_prev = jnp.zeros(upper_c.shape[1:], jnp.float32)
    value_prev = jnp.zeros((rhs.shape[0],) + upper_c.shape[1:], jnp.float32)
    for level in range(depth):
        upper = upper_c[level]
        pivot = diagonal[level] - upper * ratio_prev
        ratio_prev = lower_c[level] / pivot
        value_prev = (rhs[:, level] + upper * value_prev) / pivot
        ratios.append(ratio_prev)
        values.append(value_prev)
    solved = [None] * depth
    carry = jnp.zeros_like(value_prev)
    for level in range(depth - 1, -1, -1):
        carry = values[level] + ratios[level] * carry
        solved[level] = carry
    return jnp.stack(solved, axis=1)


def vertical(inter, tracers, cotangent, wet, background):
    density = -ALPHA_T * tracers[0] + BETA_S * tracers[1]
    wet_pair = wet[:-1] * wet[1:]
    gate = jax.nn.sigmoid(density[:-1] - density[1:])
    mix = (background[None] + MIXING * gate) * wet_pair
    zero = jnp.zeros_like(mix[:1])
    upper_c = jnp.concatenate([zero, mix], axis=0)
    lower_c = jnp.concatenate([mix, zero], axis=0)
    diagonal = 1.0 + upper_c + lower_c
    rhs = jnp.concatenate([inter, cotangent], axis=0)
    solved = solve_columns(upper_c, lower_c, diagonal, rhs)
    after = solved[:4]
    back = solved[4:]
    coef_grad = -jnp.sum((back[:, :-1] - back[:, 1:]) * (after[:, :-1] - after[:, 1:]), axis=0)
    back_grad = jnp.sum(coef_grad * wet_pair, axis=0)
    slope = coef_grad * MIXING * gate * (1.0 - gate) * wet_pair
    dens_grad = jnp.concatenate([slope, zero], axis=0) - jnp.concatenate([zero, slope], axis=0)
    tracer_grad = jnp.stack([-ALPHA_T * dens_grad * wet, BETA_S * dens_grad * wet], axis=0)
    return (back, tracer_grad, back_grad)


def shards(state, cotangent, land_mask, wet_count, background):
    stores = lax.axis_size("store")
    store_id = lax.axis_index("store")
    slab = state.shape[1]
    cols = state.shape[3]
    depth = slab * stores
    part = cols // stores
    slab_ids = store_id * slab + jnp.arange(slab, dtype=jnp.int32)
    wet_slab = wet_of(land_mask, wet_count, slab_ids)
    state_pad, wet_pad = (
        padded(state, (("tile", 3),), 1),
        padded(wet_slab[None], (("tile", 3),), 1),
    )
    inter = hstep(state_pad, wet_pad)
    tracers = state[:2] * wet_slab[None]
    inter_all, tracers_all, cot_all = (
        lax.all_gather(inter, "store", axis=1, tiled=True),
        lax.all_gather(tracers, "store", axis=1, tiled=True),
        lax.all_gather(cotangent, "store", axis=1, tiled=True),
    )
    wet_all = wet_of(land_mask, wet_count, jnp.arange(depth, dtype=jnp.int32))
    back_all, tgrad_all, bgrad_all = vertical(inter_all, tracers_all, cot_all, wet_all, background)
    back = lax.dynamic_slice_in_dim(back_all, store_id * slab, slab, 1)
    tracer_grad = lax.dynamic_slice_in_dim(tgrad_all, store_id * slab, slab, 1)
    background_grad = lax.dynamic_slice_in_dim(bgrad_all, store_id * part, part, 1)
    back_pad = padded(back, (("tile", 3),), 1)
    cols_pad = ((0, 0), (0, 0), (0, 0), (1, 1))
    state_wider = jnp.pad(state_pad, cols_pad)
    wet_wider = jnp.pad(wet_pad, cols_pad)
    _, pull_slab = jax.vjp(lambda field: hstep(field, wet_wider), state_wider)
    (grad_wider,) = pull_slab(back_pad)
    grad_h = grad_wider[..., 2:-2]
    state_grad = grad_h + jnp.concatenate([tracer_grad, jnp.zeros_like(tracer_grad)], axis=0)
    return (state_grad, background_grad)


def solution(mesh):
    in_specs = (
        P(None, "store", None, "tile"),
        P(None, "store", None, "tile"),
        P(None, "tile"),
        P(None, "tile"),
        P(None, "tile"),
    )
    out_specs = (P(None, "store", None, "tile"), P(None, ("tile", "store")))
    return jax.shard_map(shards, mesh=mesh, in_specs=in_specs, out_specs=out_specs, check_vma=False)
```

profile of v0, /device:TPU:6, one launch (start us, length us, event | category | flops | bytes accessed | tf_op | source)
XLA Modules:
  0.0 152.5 jit_solution(16304264077253546404)
XLA Ops:
  7.9 0.8 and_convert_fusion
  8.8 7.1 %collective-permute-start.2 = (f32[1,8,8,1]{3,2,1,0:T(8,128)S(1)}, f32[1,8,8,1]{3,2,1,0:T(8,128)S(1)}, u32[]{:S(2)}, u32[]{:S(2)}) collective-permute-start(f32[1,8,8,1]{3,2,1,0:T(8,128)S(1)} %get-tuple-element.534), channel_id=1, source_target_pairs={{0,8},{8,16},{16,24},{24,32},{32,40},{40,48},{48,56},{56,64},{64,7... | collective-permute-start | bytes 776 | tf_op jit(solution)/shard_map/ppermute | solution.py:20
  15.9 1.1 fusion.292
  17.1 8.0 %collective-permute-start = (f32[4,8,8,1]{3,2,0,1:T(8,128)S(1)}, f32[4,8,8,1]{3,2,0,1:T(8,128)S(1)}, u32[]{:S(2)}, u32[]{:S(2)}) collective-permute-start(f32[4,8,8,1]{3,2,0,1:T(8,128)S(1)} %get-tuple-element.337), channel_id=1, source_target_pairs={{0,8},{8,16},{16,24},{24,32},{32,40},{40,48},{48,56},{56,64},{64,7... | collective-permute-start | bytes 3080 | tf_op jit(solution)/shard_map/ppermute | solution.py:20
  25.1 0.8 fusion.114
  25.9 0.8 fusion.113
  26.9 0.7 collective-permute-done
  27.6 8.6 %collective-permute-done.1 = f32[4,8,8,1]{3,2,0,1:T(8,128)S(1)} collective-permute-done((f32[4,8,8,1]{3,2,0,1:T(8,128)S(1)}, f32[4,8,8,1]{3,2,0,1:T(8,128)S(1)}, u32[]{:S(2)}, u32[]{:S(2)}) %collective-permute-start.1) | collective-permute-done | bytes 1056 | tf_op jit(solution)/shard_map/ppermute | solution.py:22
  36.2 1.1 broadcast_multiply_fusion
  37.6 0.8 fusion.18
  39.2 16.3 %all_gather.11 = f32[2,64,8,128]{3,2,1,0:T(8,128)S(1)} all-gather(f32[2,8,8,128]{3,2,1,0:T(8,128)S(1)} %slice_multiply_fusion.6), channel_id=1, replica_groups=mesh['tile'=32,'store'=8] {'store'}, dimensions={1}, use_global_device_ids=true | all-gather | bytes 589824 | tf_op jit(solution)/shard_map/all_gather | solution.py:132
  83.6 1.3 divide_multiply_fusion.43
  85.1 0.7 slice.1252
  86.3 0.8 slice_bitcast_fusion.1
  87.0 1.3 constant_dynamic-update-slice_fusion.1
  88.3 26.7 %all-gather.5.cloned.1.call-done = f32[4,64,8,128]{3,2,0,1:T(8,128)} async-done(((f32[4,8,8,128]{3,2,0,1:T(8,128)}), f32[4,64,8,128]{3,2,0,1:T(8,128)}) %all-gather.5.cloned.1.call-update) | async-done | bytes 1048592 | tf_op jit(solution)/shard_map/all_gather | solution.py:133
  115.4 1.3 constant_dynamic-update-slice_fusion
  117.1 1.3 add_divide_fusion
  118.8 1.8 %fusion.52 = (f32[8,8,128]{2,1,0:T(8,128)S(1)}, f32[8,8,128]{2,1,0:T(8,128)S(1)}, f32[8,8,128]{2,1,0:T(8,128)S(1)}, f32[8,8,128]{2,1,0:T(8,128)S(1)}, f32[8,8,12...) fusion(f32[8,64,8,128]{3,2,0,1:T(8,128)S(1)} %constant_dynamic-, ...), kind=kLoop, calls=%fused_computation.301 | loop fusion | flops 1507328 | bytes 3190784 | tf_op jit(solution)/shard_map/div | solution.py:83
  121.0 1.8 %constant_dynamic-update-slice_fusion.128 = (f32[8,63,8,128]{3,2,0,1:T(8,128)S(1)}, f32[8,8,128]{2,1,0:T(8,128)S(1)}, f32[8,8,128]{2,1,0:T(8,128)S(1)}, f32[8,8,...) fusion(f32[8,8,128]{2,1,0:T(8,128)S(1)} %get-tuple-element.245,, ...), kind=kLoop, calls=%fused_computation.140 | loop fusion | flops 2105343 | bytes 3469312
  122.8 2.3 %constant_dynamic-update-slice_fusion.127 = (f32[8,63,8,128]{3,2,0,1:T(8,128)S(1)}, f32[8,1,8,128]{3,2,0,1:T(8,128)S(1)}, f32[8,1,8,128]{3,2,0,1:T(8,128)S(1)}, ...) fusion(f32[8,63,8,128]{3,2,0,1:T(8,128)S(1)} %get-tuple-element, ...), kind=kLoop, calls=%fused_computation.139 | loop fusion | flops 2056192 | bytes 4075520
  127.4 3.3 %collective-permute-start.4 = (f32[4,8,8,1]{3,2,0,1:T(8,128)S(1)}, f32[4,8,8,1]{3,2,0,1:T(8,128)S(1)}, u32[]{:S(2)}, u32[]{:S(2)}) collective-permute-start(f32[4,8,8,1]{3,2,0,1:T(8,128)S(1)} %get-tuple-element.248), channel_id=1, source_target_pairs={{0,8},{8,16},{16,24},{24,32},{32,40},{40,48},{48,56},{56,64},{64,7... | collective-permute-start | bytes 3080 | tf_op jit(solution)/shard_map/ppermute | solution.py:20
  131.3 3.2 %collective-permute-done.4 = f32[4,8,8,1]{3,2,0,1:T(8,128)S(1)} collective-permute-done((f32[4,8,8,1]{3,2,0,1:T(8,128)S(1)}, f32[4,8,8,1]{3,2,0,1:T(8,128)S(1)}, u32[]{:S(2)}, u32[]{:S(2)}) %collective-permute-start.4) | collective-permute-done | bytes 1056 | tf_op jit(solution)/shard_map/ppermute | solution.py:20
  134.5 9.3 %collective-permute-done.5 = f32[4,8,8,1]{3,2,0,1:T(8,128)S(1)} collective-permute-done((f32[4,8,8,1]{3,2,0,1:T(8,128)S(1)}, f32[4,8,8,1]{3,2,0,1:T(8,128)S(1)}, u32[]{:S(2)}, u32[]{:S(2)}) %collective-permute-start.5) | collective-permute-done | bytes 1056 | tf_op jit(solution)/shard_map/ppermute | solution.py:22
  (419 shorter events, 35.1 us)
Async XLA Ops:
  7.2 31.3 %copy-start.36 = (f32[4,8,8,128]{3,2,1,0:T(8,128)S(1)}, f32[4,8,8,128]{3,2,1,0:T(8,128)}, u32[]{:S(2)}) copy-start(f32[4,8,8,128]{3,2,1,0:T(8,128)} %param.6) | copy-start | bytes 393220
  7.2 79.8 %all-gather.3.cloned.1.call-start = ((), (), s32[]{:S(2)}) async-start(), calls=%async_computation | async-start | bytes 1179648 | tf_op jit(solution)/shard_map/all_gather | solution.py:131
  7.9 31.2 %copy-start.125 = (pred[8,128]{1,0:T(8,128)(4,1)}, pred[8,128]{1,0:T(8,128)(4,1)S(1)}, u32[]{:S(2)}) copy-start(pred[8,128]{1,0:T(8,128)(4,1)S(1)} %broadcast_compare_fusion) | copy-start | bytes 3076
  8.8 17.9 %collective-permute-start.2 = (f32[1,8,8,1]{3,2,1,0:T(8,128)S(1)}, f32[1,8,8,1]{3,2,1,0:T(8,128)S(1)}, u32[]{:S(2)}, u32[]{:S(2)}) collective-permute-start(f32[1,8,8,1]{3,2,1,0:T(8,128)S(1)} %get-tuple-element.534), channel_id=1, source_target_pairs={{0,8},{8,16},{16,24},{24,32},{32,40},{40,48},{48,56},{56,64},{64,7... | collective-permute-start | bytes 776 | tf_op jit(solution)/shard_map/ppermute | solution.py:20
  15.9 23.2 %copy-start = (f32[4,8,8,128]{3,2,1,0:T(8,128)S(1)}, f32[4,8,8,128]{3,2,1,0:T(8,128)}, u32[]{:S(2)}) copy-start(f32[4,8,8,128]{3,2,1,0:T(8,128)} %param.5) | copy-start | bytes 393220
  15.9 10.8 %collective-permute-start.3 = (f32[1,8,8,1]{3,2,1,0:T(8,128)S(1)}, f32[1,8,8,1]{3,2,1,0:T(8,128)S(1)}, u32[]{:S(2)}, u32[]{:S(2)}) collective-permute-start(f32[1,8,8,1]{3,2,1,0:T(8,128)S(1)} %get-tuple-element.535), channel_id=1, source_target_pairs={{8,0},{16,8},{24,16},{32,24},{40,32},{48,40},{56,48},{64,56},{72,6... | collective-permute-start | bytes 776 | tf_op jit(solution)/shard_map/ppermute | solution.py:22
  17.1 22.1 %copy-start.81 = (s32[8,128]{1,0:T(8,128)S(1)}, s32[8,128]{1,0:T(8,128)}, u32[]{:S(2)}) copy-start(s32[8,128]{1,0:T(8,128)} %param.8) | copy-start | bytes 12292
  17.1 10.6 %collective-permute-start = (f32[4,8,8,1]{3,2,0,1:T(8,128)S(1)}, f32[4,8,8,1]{3,2,0,1:T(8,128)S(1)}, u32[]{:S(2)}, u32[]{:S(2)}) collective-permute-start(f32[4,8,8,1]{3,2,0,1:T(8,128)S(1)} %get-tuple-element.337), channel_id=1, source_target_pairs={{0,8},{8,16},{16,24},{24,32},{32,40},{40,48},{48,56},{56,64},{64,7... | collective-permute-start | bytes 3080 | tf_op jit(solution)/shard_map/ppermute | solution.py:20
  25.1 11.1 %collective-permute-start.1 = (f32[4,8,8,1]{3,2,0,1:T(8,128)S(1)}, f32[4,8,8,1]{3,2,0,1:T(8,128)S(1)}, u32[]{:S(2)}, u32[]{:S(2)}) collective-permute-start(f32[4,8,8,1]{3,2,0,1:T(8,128)S(1)} %get-tuple-element.338), channel_id=1, source_target_pairs={{8,0},{16,8},{24,16},{32,24},{40,32},{48,40},{56,48},{64,56},{72,6... | collective-permute-start | bytes 3080 | tf_op jit(solution)/shard_map/ppermute | solution.py:22
  26.7 28.9 %copy-start.128 = (f32[8]{0:T(128)}, f32[8]{0:T(128)S(1)}, u32[]{:S(2)}) copy-start(f32[8]{0:T(128)S(1)} %get-tuple-element.536) | copy-start | bytes 100
  26.7 28.9 %copy-start.130 = (f32[8]{0:T(128)}, f32[8]{0:T(128)S(1)}, u32[]{:S(2)}) copy-start(f32[8]{0:T(128)S(1)} %get-tuple-element.537) | copy-start | bytes 100
  37.3 18.4 %copy-start.127 = (f32[8,128]{1,0:T(8,128)S(1)}, f32[8,128]{1,0:T(8,128)}, u32[]{:S(2)}) copy-start(f32[8,128]{1,0:T(8,128)} %param.9) | copy-start | bytes 12292
  38.4 76.6 %all-gather.5.cloned.1.call-start = ((), (), s32[]{:S(2)}) async-start(), calls=%async_computation.1 | async-start | bytes 1179648 | tf_op jit(solution)/shard_map/all_gather | solution.py:133
  61.8 21.7 %copy-start.3 = (f32[1,8,128]{2,1,0:T(8,128)}, f32[1,8,128]{2,1,0:T(8,128)S(1)}, u32[]{:S(2)}) copy-start(f32[1,8,128]{2,1,0:T(8,128)S(1)} %get-tuple-element.120) | copy-start | bytes 12292
  63.1 20.4 %copy-start.5 = (f32[1,8,128]{2,1,0:T(8,128)}, f32[1,8,128]{2,1,0:T(8,128)S(1)}, u32[]{:S(2)}) copy-start(f32[1,8,128]{2,1,0:T(8,128)S(1)} %get-tuple-element.124) | copy-start | bytes 12292
  64.3 19.2 %copy-start.7 = (f32[1,8,128]{2,1,0:T(8,128)}, f32[1,8,128]{2,1,0:T(8,128)S(1)}, u32[]{:S(2)}) copy-start(f32[1,8,128]{2,1,0:T(8,128)S(1)} %get-tuple-element.128) | copy-start | bytes 12292
  65.5 18.0 %copy-start.9 = (f32[1,8,128]{2,1,0:T(8,128)}, f32[1,8,128]{2,1,0:T(8,128)S(1)}, u32[]{:S(2)}) copy-start(f32[1,8,128]{2,1,0:T(8,128)S(1)} %get-tuple-element.132) | copy-start | bytes 12292
  66.7 16.8 %copy-start.11 = (f32[1,8,128]{2,1,0:T(8,128)}, f32[1,8,128]{2,1,0:T(8,128)S(1)}, u32[]{:S(2)}) copy-start(f32[1,8,128]{2,1,0:T(8,128)S(1)} %get-tuple-element.136) | copy-start | bytes 12292
  127.1 16.9 %copy-start.1 = (f32[8,8,130]{2,1,0:T(8,128)S(1)}, f32[8,8,130]{2,1,0:T(8,128)}, u32[]{:S(2)}) copy-start(f32[8,8,130]{2,1,0:T(8,128)} %get-tuple-element.265) | copy-start | bytes 99844
  127.1 16.9 %copy-start.2 = (f32[8,8,130]{2,1,0:T(8,128)S(1)}, f32[8,8,130]{2,1,0:T(8,128)}, u32[]{:S(2)}) copy-start(f32[8,8,130]{2,1,0:T(8,128)} %get-tuple-element.266) | copy-start | bytes 99844
  127.2 16.9 %copy-start.129 = (f32[8]{0:T(128)S(1)}, f32[8]{0:T(128)}, u32[]{:S(2)}) copy-start(f32[8]{0:T(128)} %copy-done.128) | copy-start | bytes 100
  127.2 16.9 %copy-start.131 = (f32[8]{0:T(128)S(1)}, f32[8]{0:T(128)}, u32[]{:S(2)}) copy-start(f32[8]{0:T(128)} %copy-done.130) | copy-start | bytes 100
  127.4 7.1 %collective-permute-start.4 = (f32[4,8,8,1]{3,2,0,1:T(8,128)S(1)}, f32[4,8,8,1]{3,2,0,1:T(8,128)S(1)}, u32[]{:S(2)}, u32[]{:S(2)}) collective-permute-start(f32[4,8,8,1]{3,2,0,1:T(8,128)S(1)} %get-tuple-element.248), channel_id=1, source_target_pairs={{0,8},{8,16},{16,24},{24,32},{32,40},{40,48},{48,56},{56,64},{64,7... | collective-permute-start | bytes 3080 | tf_op jit(solution)/shard_map/ppermute | solution.py:20
  130.7 13.1 %collective-permute-start.5 = (f32[4,8,8,1]{3,2,0,1:T(8,128)S(1)}, f32[4,8,8,1]{3,2,0,1:T(8,128)S(1)}, u32[]{:S(2)}, u32[]{:S(2)}) collective-permute-start(f32[4,8,8,1]{3,2,0,1:T(8,128)S(1)} %get-tuple-element.249), channel_id=1, source_target_pairs={{8,0},{16,8},{24,16},{32,24},{40,32},{48,40},{56,48},{64,56},{72,6... | collective-permute-start | bytes 3080 | tf_op jit(solution)/shard_map/ppermute | solution.py:22
  (116 other events, 305.5 us)
Sparse Core Ops, SparseCore 0:
  38.5 38.9 all-gather.2
  79.3 35.6 all-gather.4
where the time goes:
time: 153 us
  waiting for transfers between devices  48.5 us (32%)
  other arithmetic  42.2 us (28%)
  starting transfers between devices  18.6 us (12%)
  between operations  16.4 us (11%)
  blocking collectives  16.3 us (11%)
  local copies, waits for them, and re-layouts  10.6 us (7%)
    mul x44, other arithmetic, solve_columns(): carry = values[level] + ratios[level] * carry  27.5 us
    all_gather x1, waiting for transfers between devices, shards(): lax.all_gather(cotangent, 'store', axis=1, tiled=True)  26.7 us
    ppermute x3, starting transfers between devices, padded(): lax.ppermute(tail, axis, [(i, (i + 1) % count) for i in range(count)])  18.5 us
    ppermute x3, waiting for transfers between devices, padded(): lax.ppermute(head, axis, [((i + 1) % count, i) for i in range(count)])  17.8 us
    all_gather x1, blocking collectives, shards(): lax.all_gather(tracers, 'store', axis=1, tiled=True)  16.3 us
    unnamed x2, other arithmetic  4.06 us
    unnamed x329, local copies, waits for them, and re-layouts  4.03 us
    ppermute x3, waiting for transfers between devices, padded(): lax.ppermute(tail, axis, [(i, (i + 1) % count) for i in range(count)])  3.89 us
  transfers between devices with their start and end apart: 8, of which 5 were waited for; matrix products, arithmetic and copies ran while one was open for 24% of the time, Pallas kernels for 0%

commit v1 on v0

v1 whole, which is shorter than its diff:
```python
import functools

import jax
import jax.numpy as jnp
from jax import lax
from jax.experimental import pallas as pl
from jax.experimental.pallas import tpu as pltpu
from jax.sharding import PartitionSpec as P

DIFFUSE = 0.1
ADVECT = 0.05
MIXING = 2.0
ALPHA_T = 0.6
BETA_S = 0.8
MESH = pl.DeviceIdType.MESH
F32 = jnp.float32


def lanes(x, shift):
    shift %= 128
    return pltpu.roll(x, shift, x.ndim - 1) if shift else x


def rows(x, shift):
    return pltpu.roll(x, shift % 8, x.ndim - 2)


def kernel(
    n_tile, n_store, state_h, cot_h, land_h, count_h, bg_h, out, bg_out,
    st, ct, land, count, bg,
    edge, edge_rx, bedge, bedge_rx, dens_tx, dens_rx,
    early, early_rx, ret1, ret1_rx, late, late_rx, ret2, ret2_rx, part, part_rx,
    in_sem, edge_s, edge_r, bedge_s, bedge_r, dens_s, dens_r,
    early_s, early_r, ret1_s, ret1_r, late_s, late_r, ret2_s, ret2_r, part_s, part_r,
):
    t = lax.axis_index("tile")
    s = lax.axis_index("store")
    east = lax.rem(t + 1, n_tile)
    west = lax.rem(t + n_tile - 1, n_tile)
    below = lax.rem(s + 1, n_store)
    above = lax.rem(s + n_store - 1, n_store)

    barrier = pltpu.get_barrier_semaphore()
    for d in range(1, n_store):
        pl.semaphore_signal(barrier, inc=1, device_id={"store": lax.rem(s + d, n_store)}, device_id_type=MESH)
    for to in (east, west):
        pl.semaphore_signal(barrier, inc=1, device_id={"tile": to}, device_id_type=MESH)

    loads = [
        pltpu.make_async_copy(src, dst, in_sem.at[i])
        for i, (src, dst) in enumerate(((land_h, land), (count_h, count), (bg_h, bg), (state_h, st), (cot_h, ct)))
    ]
    for load in loads:
        load.start()

    lane = lax.broadcasted_iota(jnp.int32, (8, 128), 1)
    row = lax.broadcasted_iota(jnp.int32, (8, 128), 0)
    block = lane >> 4
    pairs = ((lane + 1) & 127) >> 1
    first = lane == 0
    last = lane == 127

    def send(src, dst, send_sem, recv_sem, where):
        return pltpu.make_async_remote_copy(
            src_ref=src, dst_ref=dst, send_sem=send_sem, recv_sem=recv_sem, device_id=where, device_id_type=MESH
        )

    def mates(src, dst, send_sem, recv_sem):
        copies = []
        for d in range(1, n_store):
            to = lax.rem(s + d, n_store)
            copies.append(send(src(to), dst.at[s], send_sem.at[d - 1], recv_sem.at[d - 1], {"store": to}))
        return copies

    def start(copies):
        for copy in copies:
            copy.start()

    def arrived(copies):
        for copy in copies:
            copy.wait_recv()

    def exchange_blocks(tiles):
        tiles = list(tiles)
        for b in (4, 2, 1):
            keep = (block & b) == 0
            new = [None] * 8
            for v in range(8):
                if v & b == 0:
                    lo, hi = tiles[v], tiles[v + b]
                    new[v] = jnp.where(keep, lo, lanes(hi, 16 * b))
                    new[v + b] = jnp.where(keep, lanes(lo, -16 * b), hi)
            tiles = new
        return tiles

    def pack_edges(tiles):
        half = tiles.shape[0] // 2
        while half:
            tiles = jnp.where((pairs & half) != 0, lanes(tiles[half:], 2 * half), tiles[:half])
            half //= 2
        return tiles[0]

    def unpack_edges(from_west, from_east):
        both = lanes(jnp.where((lane & 1) == 0, from_east, lanes(from_west, 2)), 127)
        spread = both[None]
        for half in (1, 2, 4, 8, 16):
            spread = jnp.concatenate([spread, lanes(spread, -2 * half)], axis=0)
        return spread.reshape(4, 8, 8, 128), lanes(both, -64)

    def to_east(x, halo):
        return jnp.where(last, halo, lanes(x, 127))

    def to_west(x, halo):
        return jnp.where(first, halo, lanes(x, 1))

    def to_north(x):
        return jnp.where(row == 7, 0.0, rows(x, 7))

    def to_south(x):
        return jnp.where(row == 0, 0.0, rows(x, 1))

    level = (lax.broadcasted_iota(jnp.int32, (8, 8, 128), 0) + s * 8).astype(F32)
    base = (s * 8).astype(F32)

    for load in loads[:3]:
        load.wait()
    depth = jnp.where(land[...] == 1, count[...], 0).astype(F32)
    wet = jnp.where(level < depth, 1.0, 0.0)
    backgr = bg[...]

    loads[3].wait()
    masked = st[...] * wet
    edges = pack_edges(masked.reshape(32, 8, 128))
    edge[...] = jnp.where(pairs == 32, lanes(depth, 64), edges)

    density = -ALPHA_T * masked[0] + BETA_S * masked[1]
    dens_tx[0] = density[7]
    dens_tx[1] = density[0]
    gate = jax.nn.sigmoid(density[:-1] - density[1:])
    pair = wet[1:]
    mix = (backgr + MIXING * gate) * pair
    ratio = []
    inverse = []
    excess = jnp.ones((8, 128), F32)
    for i in range(8):
        if i < 7:
            inv = 1.0 / (excess + mix[i])
            ratio.append(mix[i] * inv)
            inverse.append(inv)
            excess = 1.0 + ratio[i] * excess
        else:
            inverse.append(1.0 / excess)

    def local_solve(rhs):
        values = [rhs[0] * inverse[0]]
        for i in range(1, 8):
            values.append((rhs[i] + mix[i - 1] * values[-1]) * inverse[i])
        for i in range(6, -1, -1):
            values[i] = values[i] + ratio[i] * values[i + 1]
        return values

    up = [inverse[0]]
    for i in range(1, 8):
        up.append(mix[i - 1] * up[-1] * inverse[i])
    for i in range(6, -1, -1):
        up[i] = up[i] + ratio[i] * up[i + 1]
    down = [None] * 7 + [inverse[7]]
    for i in range(6, -1, -1):
        down[i] = ratio[i] * down[i + 1]

    loads[4].wait()
    p_back = local_solve([ct[:, i] for i in range(8)])
    bottom_wet = base + 8.0 < depth
    bg_pair = jnp.where(bottom_wet, backgr, 0.0)
    ends = [p_back[0][f] for f in range(4)] + [p_back[7][f] for f in range(4)]
    for d, tile in enumerate(exchange_blocks(ends)):
        early[d, 0] = tile
    matrix = [up[0], up[7], down[7], density[0], density[7], bg_pair, bg_pair, bg_pair]
    for d, tile in enumerate(exchange_blocks(matrix)):
        early[d, 1] = tile
    early_rx[s] = early[s]

    pl.semaphore_wait(barrier, n_store - 1 + 2)
    edge_copies = [
        send(edge, edge_rx.at[0], edge_s.at[0], edge_r.at[0], {"tile": east}),
        send(edge, edge_rx.at[1], edge_s.at[1], edge_r.at[1], {"tile": west}),
    ]
    start(edge_copies)
    early_copies = mates(lambda to: early.at[to], early_rx, early_s, early_r)
    start(early_copies)
    dens_copies = [
        send(dens_tx.at[0], dens_rx.at[0], dens_s.at[0], dens_r.at[0], {"store": below}),
        send(dens_tx.at[1], dens_rx.at[1], dens_s.at[1], dens_r.at[1], {"store": above}),
    ]
    start(dens_copies)

    arrived(early_copies)
    m_inv, low, high = [], [], []
    ends_rx = [early_rx[j, 0] for j in range(8)]
    mat_rx = [early_rx[j, 1] for j in range(8)]

    def four(x):
        x = jnp.where(block == 0, x, lanes(x, 16))
        return jnp.where(block < 2, x, lanes(x, 32))

    prev = None
    for j in range(7):
        here, there = mat_rx[j], mat_rx[j + 1]
        jump = lanes(here, -64) - lanes(there, -48)
        weight = lanes(here, -80)
        m = jnp.where(weight > 0.0, weight + MIXING * jax.nn.sigmoid(jump), 0.0)
        pivot = 1.0 + m * (lanes(here, -32) + there)
        lower = m * lanes(here, -16)
        if j:
            pivot = pivot - lower * prev
        pivot = jnp.where(block == 0, pivot, 1.0)
        inv = 1.0 / pivot
        prev = m * lanes(there, -16) * inv
        m_inv.append(four(m * inv))
        low.append(four(lower * inv))
        high.append(four(prev))

    def fluxes(tiles):
        flux = []
        for j in range(7):
            value = m_inv[j] * (lanes(tiles[j], 64) - tiles[j + 1])
            flux.append(value + low[j] * flux[-1] if j else value)
        for j in range(5, -1, -1):
            flux[j] = flux[j] + high[j] * flux[j + 1]
        return flux

    def returns(flux, ref):
        left = lane < 64
        for d in range(8):
            above_flux = flux[d - 1] if d else 0.0
            below_flux = lanes(flux[d], 64) if d < 7 else 0.0
            ref[d] = jnp.where(left, above_flux, below_flux)

    returns(fluxes(ends_rx), ret1)
    ret1_rx[s] = ret1[s]
    ret1_copies = mates(lambda to: ret1.at[to], ret1_rx, ret1_s, ret1_r)
    start(ret1_copies)

    arrived(edge_copies)
    halo, depth_halo = unpack_edges(edge_rx[0], edge_rx[1])
    around = jnp.where(level < to_east(depth, depth_halo), 1.0, 0.0)
    around += jnp.where(level < to_west(depth, depth_halo), 1.0, 0.0)
    around += jnp.where(level < to_north(depth), 1.0, 0.0)
    around += jnp.where(level < to_south(depth), 1.0, 0.0)
    centre = wet * (1.0 - DIFFUSE * around)
    spread = DIFFUSE * wet
    m_east = to_east(masked, halo)
    m_west = to_west(masked, halo)
    m_north = to_north(masked)
    m_south = to_south(masked)
    latitude = 0.1 + 0.2 * (row.astype(F32) + 0.5) / 8.0
    inter = centre * masked + spread * (m_east + m_west + m_north + m_south)
    zonal, merid = masked[2], masked[3]
    grad_x = m_east[:2] - m_west[:2]
    grad_y = m_north[:2] - m_south[:2]
    advect = -ADVECT * (zonal * grad_x + merid * grad_y)
    rhs = [inter[0] + advect[0], inter[1] + advect[1], inter[2] + latitude * merid, inter[3] - latitude * zonal]
    rhs = jnp.stack(rhs, axis=1)
    p_after = local_solve([rhs[i] for i in range(8)])
    ends = [p_after[0][f] for f in range(4)] + [p_after[7][f] for f in range(4)]
    for d, tile in enumerate(exchange_blocks(ends)):
        late[d] = tile
    late_rx[s] = late[s]
    late_copies = mates(lambda to: late.at[to], late_rx, late_s, late_r)
    start(late_copies)

    arrived(ret1_copies)
    flux_b = exchange_blocks([ret1_rx[d] for d in range(8)])
    top_b = jnp.stack(flux_b[:4])
    bot_b = jnp.stack(flux_b[4:])
    back = jnp.stack([p_back[i] + up[i] * top_b - down[i] * bot_b for i in range(8)], axis=1)
    wet_back = wet * back
    bedge[...] = pack_edges(wet_back.reshape(32, 8, 128))
    bedge_copies = [
        send(bedge, bedge_rx.at[0], bedge_s.at[0], bedge_r.at[0], {"tile": east}),
        send(bedge, bedge_rx.at[1], bedge_s.at[1], bedge_r.at[1], {"tile": west}),
    ]
    start(bedge_copies)

    arrived(late_copies)
    returns(fluxes([late_rx[j] for j in range(8)]), ret2)
    ret2_rx[s] = ret2[s]
    ret2_copies = mates(lambda to: ret2.at[to], ret2_rx, ret2_s, ret2_r)
    start(ret2_copies)

    arrived(dens_copies)
    gate_top = jax.nn.sigmoid(dens_rx[0] - density[0])
    gate_bot = jax.nn.sigmoid(density[7] - dens_rx[1])
    pair_top = jnp.where(base > 0.0, wet[0], 0.0)
    pair_bot = jnp.where(bottom_wet, 1.0, 0.0)
    scale_top = pair_top / (backgr + MIXING * gate_top)
    scale_bot = pair_bot / (backgr + MIXING * gate_bot)

    arrived(ret2_copies)
    flux_a = exchange_blocks([ret2_rx[d] for d in range(8)])
    top_a = jnp.stack(flux_a[:4])
    bot_a = jnp.stack(flux_a[4:])
    after = jnp.stack([p_after[i] + up[i] * top_a - down[i] * bot_a for i in range(8)], axis=1)
    coef = -jnp.sum((back[:, :-1] - back[:, 1:]) * (after[:, :-1] - after[:, 1:]), axis=0) * pair
    coef_top = -jnp.sum(top_b * top_a, axis=0) * (scale_top * scale_top)
    coef_bot = -jnp.sum(bot_b * bot_a, axis=0) * (scale_bot * scale_bot)
    total = jnp.sum(coef, axis=0) + coef_bot
    part[...] = total
    part_rx[s] = total
    part_copies = mates(lambda to: part, part_rx, part_s, part_r)
    start(part_copies)
    slope = MIXING * coef * gate * (1.0 - gate)
    slope_top = MIXING * coef_top * gate_top * (1.0 - gate_top)
    slope_bot = MIXING * coef_bot * gate_bot * (1.0 - gate_bot)
    dens_grad = jnp.concatenate([slope, slope_bot[None]], axis=0) - jnp.concatenate([slope_top[None], slope], axis=0)

    b_north = to_north(wet_back)
    b_south = to_south(wet_back)
    arrived(bedge_copies)
    b_halo, _ = unpack_edges(bedge_rx[0], bedge_rx[1])
    b_east = to_east(wet_back, b_halo)
    b_west = to_west(wet_back, b_halo)
    grad = centre * wet_back + spread * (b_east + b_west + b_north + b_south)
    flow = m_east[2] * b_east[:2] - m_west[2] * b_west[:2] + m_north[3] * b_north[:2] - m_south[3] * b_south[:2]
    tracer = ADVECT * flow
    out[0] = grad[0] + wet * (tracer[0] - ALPHA_T * dens_grad)
    out[1] = grad[1] + wet * (tracer[1] + BETA_S * dens_grad)
    out[2] = grad[2] - ADVECT * jnp.sum(wet_back[:2] * grad_x, axis=0) - latitude * wet_back[3]
    out[3] = grad[3] - ADVECT * jnp.sum(wet_back[:2] * grad_y, axis=0) + latitude * wet_back[2]

    arrived(part_copies)
    bg_out[...] = jnp.sum(part_rx[...], axis=0)
    for copies in (edge_copies, early_copies, dens_copies, ret1_copies, late_copies, bedge_copies, ret2_copies, part_copies):
        for copy in copies:
            copy.wait_send()


def shards(n_tile, n_store, state, cotangent, land_mask, wet_count, background):
    tile = (8, 128)
    vmem = functools.partial(pltpu.VMEM, dtype=F32)
    sem = pltpu.SemaphoreType.DMA
    mates = n_store - 1
    grad, bg_sum = pl.pallas_call(
        functools.partial(kernel, n_tile, n_store),
        name="ocean",
        out_shape=(jax.ShapeDtypeStruct(state.shape, F32), jax.ShapeDtypeStruct(tile, F32)),
        in_specs=[pl.BlockSpec(memory_space=pl.ANY)] * 5,
        out_specs=(pl.BlockSpec(memory_space=pltpu.VMEM), pl.BlockSpec(memory_space=pltpu.VMEM)),
        scratch_shapes=[
            vmem(state.shape), vmem(state.shape),
            pltpu.VMEM(tile, jnp.int32), pltpu.VMEM(tile, jnp.int32), vmem(tile),
            vmem(tile), vmem((2,) + tile), vmem(tile), vmem((2,) + tile), vmem((2,) + tile), vmem((2,) + tile),
            vmem((n_store, 2) + tile), vmem((n_store, 2) + tile),
            vmem((n_store,) + tile), vmem((n_store,) + tile),
            vmem((n_store,) + tile), vmem((n_store,) + tile),
            vmem((n_store,) + tile), vmem((n_store,) + tile),
            vmem(tile), vmem((n_store,) + tile),
            sem((5,)), sem((2,)), sem((2,)), sem((2,)), sem((2,)), sem((2,)), sem((2,)),
        ] + [sem((mates,))] * 10,
        compiler_params=pltpu.CompilerParams(collective_id=0, has_side_effects=True),
    )(state, cotangent, land_mask, wet_count, background)
    part = state.shape[3] // n_store
    return grad, lax.dynamic_slice_in_dim(bg_sum, lax.axis_index("store") * part, part, 1)


def solution(mesh):
    in_specs = (
        P(None, "store", None, "tile"),
        P(None, "store", None, "tile"),
        P(None, "tile"),
        P(None, "tile"),
        P(None, "tile"),
    )
    out_specs = (P(None, "store", None, "tile"), P(None, ("tile", "store")))
    body = functools.partial(shards, mesh.shape["tile"], mesh.shape["store"])
    return jax.shard_map(body, mesh=mesh, in_specs=in_specs, out_specs=out_specs, check_vma=False)
```

time: 153 us -> 34.5 us (0.23)
  the two profiles are of different devices: /device:TPU:6 before, /device:TPU:1 now
where the time goes in v1:
time: 34.5 us; the launch traced here: 34.4 us
  Pallas kernels  30.8 us (89%)
  local copies, waits for them, and re-layouts  2.92 us (8%)
  between operations  0.64 us (2%)
    pallas_call x1, Pallas kernels, shards(): pl.pallas_call(functools.partial(kernel, n_tile, n_store), name='ocean',...  30.8 us
    unnamed x1, local copies, waits for them, and re-layouts  1.57 us
    dynamic_slice x1, local copies, waits for them, and re-layouts, shards(): lax.dynamic_slice_in_dim(bg_sum, lax.axis_index('store') * part, part, 1)  1.36 us

profile of v1, /device:TPU:1, one launch (start us, length us, event | category | flops | bytes accessed | tf_op | source)
XLA Modules:
  0.0 34.4 jit_solution(6114700871072928610)
XLA Ops:
  0.6 30.8 %ocean.1 = (f32[4,8,8,128]{3,2,1,0:T(8,128)}, f32[8,128]{1,0:T(8,128)}) custom-call(f32[4,8,8,128]{3,2,1,0:T(8,128)} %state_h.1, f32[4,8,8,128]{3,2,1,0:T(8,128)} %cot_h.1, s32[8,128]{1,0:T(8,128)} %land_h.1, s32[8,128]{1,0:T(8,128)} %count_h.1, f32[8,128]{1,0:T(8,128)} %bg_h.1), custom_call_target="tpu_custom_call" | custom-call | tf_op jit(solution)/shard_map/ocean/pallas_call | solution.py:343
  31.5 1.4 %constant_dynamic-slice_fusion = f32[8,16]{1,0:T(8,128)} fusion(f32[8,128]{1,0:T(8,128)} %get-tuple-element.5, s32[]{:T(128)S(6)} %select_n.3), kind=kLoop, calls=%fused_computation | loop fusion | bytes 1028 | tf_op jit(solution)/shard_map/dynamic_slice | solution.py:363
  32.8 1.6 %copy.8 = f32[4,8,8,128]{3,2,1,0:T(8,128)} copy(f32[4,8,8,128]{3,2,1,0:T(8,128)} %get-tuple-element.8) | data formatting | bytes 262144

commit v2 on v1

--- a/solution.py
+++ b/solution.py
@@ -31,7 +31,7 @@
     edge, edge_rx, bedge, bedge_rx, dens_tx, dens_rx,
     early, early_rx, ret1, ret1_rx, late, late_rx, ret2, ret2_rx, part, part_rx,
     in_sem, edge_s, edge_r, bedge_s, bedge_r, dens_s, dens_r,
-    early_s, early_r, ret1_s, ret1_r, late_s, late_r, ret2_s, ret2_r, part_s, part_r,
+    early_s, early_r, ret1_s, ret1_r, late_s, late_r, ret2_s, ret2_r, part_s, part_r, near, far,
 ):
     t = lax.axis_index("tile")
     s = lax.axis_index("store")
@@ -41,10 +41,21 @@
     above = lax.rem(s + n_store - 1, n_store)
 
     barrier = pltpu.get_barrier_semaphore()
-    for d in range(1, n_store):
-        pl.semaphore_signal(barrier, inc=1, device_id={"store": lax.rem(s + d, n_store)}, device_id_type=MESH)
+    core = lax.rem(s, 2)
+    chip = s - core
+    other = {"store": chip + 1 - core}
     for to in (east, west):
-        pl.semaphore_signal(barrier, inc=1, device_id={"tile": to}, device_id_type=MESH)
+        pl.semaphore_signal(barrier, inc=1, device_id={"tile": to, "store": chip + 1}, device_id_type=MESH)
+    for d in range(0, n_store, 2):
+        to = lax.rem(chip + d, n_store)
+        if d:
+            pl.semaphore_signal(barrier, inc=1, device_id={"store": to}, device_id_type=MESH)
+        else:
+
+            @pl.when(core == 1)
+            def _():
+                pl.semaphore_signal(barrier, inc=1, device_id={"store": to}, device_id_type=MESH)
+
 
     loads = [
         pltpu.make_async_copy(src, dst, in_sem.at[i])
@@ -180,12 +191,15 @@
         early[d, 1] = tile
     early_rx[s] = early[s]
 
-    pl.semaphore_wait(barrier, n_store - 1 + 2)
-    edge_copies = [
-        send(edge, edge_rx.at[0], edge_s.at[0], edge_r.at[0], {"tile": east}),
-        send(edge, edge_rx.at[1], edge_s.at[1], edge_r.at[1], {"tile": west}),
-    ]
-    start(edge_copies)
+    @pl.when(core == 0)
+    def _():
+        pl.semaphore_wait(barrier, n_store - 1)
+        pl.semaphore_signal(near, inc=1, device_id=other, device_id_type=MESH)
+
+    @pl.when(core == 1)
+    def _():
+        pl.semaphore_wait(near, 1)
+
     early_copies = mates(lambda to: early.at[to], early_rx, early_s, early_r)
     start(early_copies)
     dens_copies = [
@@ -193,6 +207,21 @@
         send(dens_tx.at[1], dens_rx.at[1], dens_s.at[1], dens_r.at[1], {"store": above}),
     ]
     start(dens_copies)
+
+    @pl.when(core == 1)
+    def _():
+        pl.semaphore_wait(barrier, 4)
+        pl.semaphore_signal(far, inc=1, device_id=other, device_id_type=MESH)
+
+    @pl.when(core == 0)
+    def _():
+        pl.semaphore_wait(far, 1)
+
+    edge_copies = [
+        send(edge, edge_rx.at[0], edge_s.at[0], edge_r.at[0], {"tile": east}),
+        send(edge, edge_rx.at[1], edge_s.at[1], edge_r.at[1], {"tile": west}),
+    ]
+    start(edge_copies)
 
     arrived(early_copies)
     m_inv, low, high = [], [], []
@@ -356,7 +385,7 @@
             vmem((n_store,) + tile), vmem((n_store,) + tile),
             vmem(tile), vmem((n_store,) + tile),
             sem((5,)), sem((2,)), sem((2,)), sem((2,)), sem((2,)), sem((2,)), sem((2,)),
-        ] + [sem((mates,))] * 10,
+        ] + [sem((mates,))] * 10 + [pltpu.SemaphoreType.REGULAR] * 2,
         compiler_params=pltpu.CompilerParams(collective_id=0, has_side_effects=True),
     )(state, cotangent, land_mask, wet_count, background)
     part = state.shape[3] // n_store

time: 34.5 us -> 34.7 us (level)
  no operation moved by 1% of the time
where the time goes in v2:
time: 34.7 us; the launch traced here: 34.5 us
  Pallas kernels  31 us (89%)
  local copies, waits for them, and re-layouts  2.92 us (8%)
  between operations  0.64 us (2%)
    pallas_call x1, Pallas kernels, shards(): pl.pallas_call(functools.partial(kernel, n_tile, n_store), name='ocean',...  31 us
    unnamed x1, local copies, waits for them, and re-layouts  1.57 us
    dynamic_slice x1, local copies, waits for them, and re-layouts, shards(): lax.dynamic_slice_in_dim(bg_sum, lax.axis_index('store') * part, part, 1)  1.36 us

profile of v2, /device:TPU:1, one launch (start us, length us, event | category | flops | bytes accessed | tf_op | source)
XLA Modules:
  0.0 34.5 jit_solution(5857244178903381804)
XLA Ops:
  0.6 31.0 %ocean.1 = (f32[4,8,8,128]{3,2,1,0:T(8,128)}, f32[8,128]{1,0:T(8,128)}) custom-call(f32[4,8,8,128]{3,2,1,0:T(8,128)} %state_h.1, f32[4,8,8,128]{3,2,1,0:T(8,128)} %cot_h.1, s32[8,128]{1,0:T(8,128)} %land_h.1, s32[8,128]{1,0:T(8,128)} %count_h.1, f32[8,128]{1,0:T(8,128)} %bg_h.1), custom_call_target="tpu_custom_call" | custom-call | tf_op jit(solution)/shard_map/ocean/pallas_call | solution.py:372
  31.6 1.4 %constant_dynamic-slice_fusion = f32[8,16]{1,0:T(8,128)} fusion(f32[8,128]{1,0:T(8,128)} %get-tuple-element.5, s32[]{:T(128)S(6)} %select_n.3), kind=kLoop, calls=%fused_computation | loop fusion | bytes 1028 | tf_op jit(solution)/shard_map/dynamic_slice | solution.py:392
  33.0 1.6 %copy.8 = f32[4,8,8,128]{3,2,1,0:T(8,128)} copy(f32[4,8,8,128]{3,2,1,0:T(8,128)} %get-tuple-element.8) | data formatting | bytes 262144

commit v3 on v1

v3 whole, which is shorter than its diff:
```python
import functools

import jax
import jax.numpy as jnp
from jax import lax
from jax.experimental import pallas as pl
from jax.experimental.pallas import tpu as pltpu
from jax.sharding import PartitionSpec as P

DIFFUSE = 0.1
ADVECT = 0.05
MIXING = 2.0
ALPHA_T = 0.6
BETA_S = 0.8
MESH = pl.DeviceIdType.MESH
F32 = jnp.float32


def lanes(x, shift):
    shift %= 128
    return pltpu.roll(x, shift, x.ndim - 1) if shift else x


def rows(x, shift):
    return pltpu.roll(x, shift % 8, x.ndim - 2)


def kernel(
    n_tile, n_store, state_h, cot_h, land_h, count_h, bg_h, out, bg_out,
    st, ct, land, count, bg,
    xa, xb, halo_rx, far_rx, own_rx, dens_tx, dens_rx,
    early, early_rx, ret1, ret1_rx, ret2, ret2_rx, part, part_rx, edge_bg,
    in_sem, halo_s, halo_r, far_s, far_r, own_s, own_r, dens_s, dens_r,
    early_s, early_r, ret1_s, ret1_r, ret2_s, ret2_r, part_s, part_r, near, far,
):
    t = lax.axis_index("tile")
    s = lax.axis_index("store")
    east = lax.rem(t + 1, n_tile)
    west = lax.rem(t + n_tile - 1, n_tile)
    below = lax.rem(s + 1, n_store)
    above = lax.rem(s + n_store - 1, n_store)
    end = n_store - 1
    owner = jnp.logical_or(s == 0, s == end)
    late = lax.rem(t // 4, 2) == 1

    barrier = pltpu.get_barrier_semaphore()

    def greet(**where):
        pl.semaphore_signal(barrier, inc=1, device_id=where, device_id_type=MESH)

    core = lax.rem(s, 2)
    chip = s - core
    other = {"store": chip + 1 - core}
    for to in (east, west):
        greet(tile=to, store=chip + 1)
    greet(**other)
    for d in range(2, n_store, 2):
        greet(store=lax.rem(chip + d, n_store))

    @pl.when(s == 0)
    def _():
        for d in range(1, n_store, 2):
            greet(tile=west, store=d)

    @pl.when(s == end)
    def _():
        for d in range(1, n_store, 2):
            greet(tile=east, store=d)

    loads = [
        pltpu.make_async_copy(src, dst, in_sem.at[i])
        for i, (src, dst) in enumerate(((land_h, land), (count_h, count), (bg_h, bg), (state_h, st), (cot_h, ct)))
    ]
    for load in loads:
        load.start()

    lane = lax.broadcasted_iota(jnp.int32, (8, 128), 1)
    row = lax.broadcasted_iota(jnp.int32, (8, 128), 0)
    block = lane >> 4
    field = (lane & 15) >> 1
    even = (lane & 1) == 0
    pairs = ((lane + 1) & 127) >> 1
    first = lane == 0
    last = lane == 127
    edge = jnp.logical_or(first, last)

    def send(src, dst, send_sem, recv_sem, where):
        return pltpu.make_async_remote_copy(
            src_ref=src, dst_ref=dst, send_sem=send_sem, recv_sem=recv_sem, device_id=where, device_id_type=MESH
        )

    def mates(src, dst, send_sem, recv_sem):
        copies = []
        for d in range(1, n_store):
            to = lax.rem(s + d, n_store)
            copies.append(send(src(to), dst.at[s], send_sem.at[d - 1], recv_sem.at[d - 1], {"store": to}))
        return copies

    def start(copies):
        for copy in copies:
            copy.start()

    def arrived(copies):
        for copy in copies:
            copy.wait_recv()

    def exchange_blocks(tiles):
        tiles = list(tiles)
        for b in (4, 2, 1):
            keep = (block & b) == 0
            new = [None] * 8
            for v in range(8):
                if v & b == 0:
                    lo, hi = tiles[v], tiles[v + b]
                    new[v] = jnp.where(keep, lo, lanes(hi, 16 * b))
                    new[v + b] = jnp.where(keep, lanes(lo, -16 * b), hi)
            tiles = new
        return tiles

    def pack_edges(tiles, bits):
        for bit in bits:
            half = tiles.shape[0] // 2
            tiles = jnp.where((pairs & bit) != 0, lanes(tiles[half:], 2 * bit), tiles[:half])
        return jnp.where(even, tiles[0], lanes(tiles[0], 2))

    def column(x, c):
        return jnp.broadcast_to(x[:, c : c + 1], (8, 128))

    def to_north(x):
        return jnp.where(row == 7, 0.0, rows(x, 7))

    def to_south(x):
        return jnp.where(row == 0, 0.0, rows(x, 1))

    def eliminate(mix):
        ratio, inverse = [], []
        excess = jnp.ones((8, 128), F32)
        for i in range(7):
            inv = 1.0 / (excess + mix[i])
            ratio.append(mix[i] * inv)
            inverse.append(inv)
            excess = 1.0 + ratio[i] * excess
        inverse.append(1.0 / excess)
        up = [inverse[0]]
        for i in range(1, 8):
            up.append(mix[i - 1] * up[-1] * inverse[i])
        for i in range(6, -1, -1):
            up[i] = up[i] + ratio[i] * up[i + 1]
        down = [None] * 7 + [inverse[7]]
        for i in range(6, -1, -1):
            down[i] = ratio[i] * down[i + 1]
        return (mix, ratio, inverse), up, down

    def local_solve(system, rhs):
        mix, ratio, inverse = system
        values = [rhs[0] * inverse[0]]
        for i in range(1, 8):
            values.append((rhs[i] + mix[i - 1] * values[-1]) * inverse[i])
        for i in range(6, -1, -1):
            values[i] = values[i] + ratio[i] * values[i + 1]
        return values

    def edge_system(tiles, start_level, depths, backs):
        dens = -ALPHA_T * tiles + BETA_S * lanes(tiles, -2)
        for bit in (1, 2, 4):
            dens = jnp.where((field & bit) == 0, dens, lanes(dens, 2 * bit))
        wets = jnp.where(jnp.stack([start_level + i for i in range(8)]) < depths, 1.0, 0.0)
        mixes = (backs + MIXING * jax.nn.sigmoid(dens[:-1] - dens[1:])) * wets[1:]
        return dens, wets, eliminate(mixes)

    def reduce_blocks(tiles):
        m_all, m_inv, low, high = [], [], [], []
        for j in range(7):
            here, there = tiles[j], tiles[j + 1]
            weight = lanes(here, -80)
            gates = jax.nn.sigmoid(lanes(here, -64) - lanes(there, -48))
            m = jnp.where(weight > 0.0, weight + MIXING * gates, 0.0)
            pivot = 1.0 + m * (lanes(here, -32) + there)
            lower = m * lanes(here, -16)
            if j:
                pivot = pivot - lower * high[-1]
            inv = 1.0 / jnp.where(block == 0, pivot, 1.0)
            m_all.append(m)
            m_inv.append(m * inv)
            low.append(lower * inv)
            high.append(m * lanes(there, -16) * inv)
        return m_all, m_inv, low, high

    def fluxes(m_inv, low, high, jumps):
        flux = []
        for j in range(7):
            value = m_inv[j] * jumps[j]
            flux.append(value + low[j] * flux[-1] if j else value)
        for j in range(5, -1, -1):
            flux[j] = flux[j] + high[j] * flux[j + 1]
        return flux

    level = (lax.broadcasted_iota(jnp.int32, (8, 8, 128), 0) + s * 8).astype(F32)
    base = (s * 8).astype(F32)

    for load in loads:
        load.wait()
    depth = jnp.where(land[...] == 1, count[...], 0).astype(F32)
    wet = jnp.where(level < depth, 1.0, 0.0)
    backgr = bg[...]
    masked = st[...] * wet
    xa[0] = jnp.where(jnp.logical_or(lane < 32, lane >= 96), depth, lanes(backgr, 64))
    fields = [masked[f] for f in range(4)] + [ct[f] for f in range(4)]
    own_edges = pack_edges(jnp.stack([fields[f][i] for i in range(8) for f in range(8)]), (32, 16, 8, 4, 2, 1))
    xa[1] = own_edges
    xb[0] = own_edges

    far_copies = [
        send(xa, far_rx.at[s], far_s.at[0], far_r.at[s], {"tile": east, "store": 0}),
        send(xa, far_rx.at[s], far_s.at[1], far_r.at[s], {"tile": west, "store": end}),
        send(xa, halo_rx.at[0], halo_s.at[0], halo_r.at[0], {"tile": east}),
        send(xa, halo_rx.at[1], halo_s.at[1], halo_r.at[1], {"tile": west}),
    ]

    def to_neighbours():
        @pl.when(core == 1)
        def _():
            pl.semaphore_wait(barrier, 7)
            pl.semaphore_signal(far, inc=1, device_id=other, device_id_type=MESH)

        @pl.when(core == 0)
        def _():
            pl.semaphore_wait(far, 1)

        start(far_copies)

    pl.when(late)(to_neighbours)

    density = -ALPHA_T * masked[0] + BETA_S * masked[1]
    dens_tx[0] = density[7]
    dens_tx[1] = density[0]
    gate = jax.nn.sigmoid(density[:-1] - density[1:])
    pair = wet[1:]
    system, up, down = eliminate((backgr + MIXING * gate) * pair)
    p_back = local_solve(system, [ct[:, i] for i in range(8)])

    shift_e = jnp.where(last, 0.0, lanes(masked, 127))
    shift_w = jnp.where(first, 0.0, lanes(masked, 1))
    around = jnp.where(level < jnp.where(last, 0.0, lanes(depth, 127)), 1.0, 0.0)
    around += jnp.where(level < jnp.where(first, 0.0, lanes(depth, 1)), 1.0, 0.0)
    around += jnp.where(level < to_north(depth), 1.0, 0.0)
    around += jnp.where(level < to_south(depth), 1.0, 0.0)
    centre = wet * (1.0 - DIFFUSE * around)
    spread = DIFFUSE * wet
    m_north = to_north(masked)
    m_south = to_south(masked)
    latitude = 0.1 + 0.2 * (row.astype(F32) + 0.5) / 8.0
    inter = centre * masked + spread * (shift_e + shift_w + m_north + m_south)
    zonal, merid = masked[2], masked[3]
    grad_x = shift_e[:2] - shift_w[:2]
    grad_y = m_north[:2] - m_south[:2]
    advect = -ADVECT * (zonal * grad_x + merid * grad_y)
    inter = [inter[0] + advect[0], inter[1] + advect[1], inter[2] + latitude * merid, inter[3] - latitude * zonal]
    xb[1] = pack_edges(jnp.stack([inter[f][i] for i in range(8) for f in range(4)]), (32, 16, 8, 2, 1))
    inter = jnp.stack(inter)
    p_after = local_solve(system, [inter[:, i] for i in range(8)])

    bottom_wet = base + 8.0 < depth
    bg_pair = jnp.where(bottom_wet, backgr, 0.0)
    groups = (
        [p_back[0][f] for f in range(4)] + [p_back[7][f] for f in range(4)],
        [p_after[0][f] for f in range(4)] + [p_after[7][f] for f in range(4)],
        [up[0], up[7], down[7], density[0], density[7], bg_pair, bg_pair, bg_pair],
    )
    for g, group in enumerate(groups):
        for d, tile in enumerate(exchange_blocks(group)):
            early[d, g] = tile
    early_rx[s] = early[s]
    own_rx[s] = xb[...]

    @pl.when(core == 0)
    def _():
        pl.semaphore_wait(barrier, end)
        pl.semaphore_signal(near, inc=1, device_id=other, device_id_type=MESH)

    @pl.when(core == 1)
    def _():
        pl.semaphore_wait(near, 1)

    early_copies = mates(lambda to: early.at[to], early_rx, early_s, early_r)
    start(early_copies)
    dens_copies = [
        send(dens_tx.at[0], dens_rx.at[0], dens_s.at[0], dens_r.at[0], {"store": below}),
        send(dens_tx.at[1], dens_rx.at[1], dens_s.at[1], dens_r.at[1], {"store": above}),
    ]
    start(dens_copies)
    own_copies = [
        (to, send(xb, own_rx.at[s], own_s.at[k], own_r.at[s], {"store": to})) for k, to in enumerate((0, end))
    ]
    for to, copy in own_copies:
        pl.when(s != to)(copy.start)

    pl.when(jnp.logical_not(late))(to_neighbours)

    arrived(early_copies)
    _, *coefs = reduce_blocks([early_rx[j, 2] for j in range(8)])

    def four(x):
        x = jnp.where(block == 0, x, lanes(x, 16))
        return jnp.where(block < 2, x, lanes(x, 32))

    coefs = [[four(x) for x in xs] for xs in coefs]
    left = lane < 64
    for g in range(2):
        ends = [early_rx[j, g] for j in range(8)]
        flux = fluxes(*coefs, [lanes(ends[j], 64) - ends[j + 1] for j in range(7)])
        for d in range(8):
            above_flux = flux[d - 1] if d else 0.0
            below_flux = lanes(flux[d], 64) if d < 7 else 0.0
            ret1[d, g] = jnp.where(left, above_flux, below_flux)
    ret1_rx[s] = ret1[s]
    ret1_copies = mates(lambda to: ret1.at[to], ret1_rx, ret1_s, ret1_r)
    start(ret1_copies)

    arrived(dens_copies)
    gate_top = jax.nn.sigmoid(dens_rx[0] - density[0])
    gate_bot = jax.nn.sigmoid(density[7] - dens_rx[1])
    pair_top = jnp.where(base > 0.0, wet[0], 0.0)
    pair_bot = jnp.where(bottom_wet, 1.0, 0.0)
    scale_top = pair_top / (backgr + MIXING * gate_top)
    scale_bot = pair_bot / (backgr + MIXING * gate_bot)

    def coefficients(after, top_a, bot_a):
        coef = -jnp.sum(diff_b * (after[:, :-1] - after[:, 1:]), axis=0) * pair
        coef_top = -jnp.sum(top_b * top_a, axis=0) * (scale_top * scale_top)
        coef_bot = -jnp.sum(bot_b * bot_a, axis=0) * (scale_bot * scale_bot)
        return coef, coef_top, coef_bot

    def finish(p, top, bot):
        return jnp.stack([p[i] + up[i] * top - down[i] * bot for i in range(8)], axis=1)

    arrived(ret1_copies)
    flux_b = exchange_blocks([ret1_rx[d, 0] for d in range(8)])
    flux_a = exchange_blocks([ret1_rx[d, 1] for d in range(8)])
    top_b, bot_b = jnp.stack(flux_b[:4]), jnp.stack(flux_b[4:])
    top_a, bot_a = jnp.stack(flux_a[:4]), jnp.stack(flux_a[4:])
    back = finish(p_back, top_b, bot_b)
    diff_b = back[:, :-1] - back[:, 1:]
    coef, _, coef_bot = coefficients(finish(p_after, top_a, bot_a), top_a, bot_a)
    total = jnp.sum(coef, axis=0) + coef_bot
    part[...] = total
    part_rx[s] = total
    part_copies = mates(lambda to: part, part_rx, part_s, part_r)
    start(part_copies)

    mine = lax.rem(s, 2)
    ret2_copies = [
        send(ret2.at[lax.rem(s + d, n_store)], ret2_rx.at[mine], ret2_s.at[d - 1], ret2_r.at[mine],
             {"store": lax.rem(s + d, n_store)})
        for d in range(1, n_store)
    ]

    @pl.when(owner)
    def _():
        for d in range(1, n_store):
            src = lax.rem(s + d, n_store)
            send(xb, own_rx.at[src], own_s.at[0], own_r.at[src], {"store": src}).wait_recv()
        for src in range(n_store):
            send(xa, far_rx.at[src], far_s.at[0], far_r.at[src], {"tile": east}).wait_recv()
        is_own = (lane & 1) == mine
        own = exchange_blocks([own_rx[j, 0] for j in range(8)])
        inter0 = jnp.stack(exchange_blocks([own_rx[j, 1] for j in range(8)]))
        halo = exchange_blocks([far_rx[j, 1] for j in range(8)])
        both = jnp.stack([jnp.where(is_own, own[i], halo[i]) for i in range(8)])
        there = far_rx[0, 0]

        def sides(x, a, b):
            return jnp.where(even, column(x, a), column(x, b))

        depths = jnp.where(is_own, sides(depth, 0, 127), sides(there, 0, 127))
        backs = jnp.where(is_own, sides(backgr, 0, 127), sides(there, 64, 63))
        start_level = (block * 8).astype(F32)
        dens, wets, (edge_sys, e_up, e_down) = edge_system(both, start_level, depths, backs)

        def swap(x):
            return jnp.where(even, lanes(x, -1), lanes(x, 1))

        m_halo = swap(both)
        along = jnp.where(field == 0, lanes(both, -4), lanes(both, -2)) * jnp.where(even, ADVECT, -ADVECT)
        delta = DIFFUSE * wets * (m_halo - swap(wets) * both) + jnp.where(field < 2, along * m_halo, 0.0)
        rhs = jnp.where(field < 4, jnp.where(is_own, inter0 + delta, 0.0), both)
        p = local_solve(edge_sys, [rhs[i] for i in range(8)])
        weight = jnp.where(start_level + 8.0 < depths, backs, 0.0)
        blocks = exchange_blocks([e_up[0], e_up[7], e_down[7], dens[0], dens[7], weight, p[0], p[7]])
        m_all, *e_coefs = reduce_blocks(blocks)
        flux = fluxes(*e_coefs, [lanes(blocks[j], -112) - lanes(blocks[j + 1], -96) for j in range(7)])
        for d in range(8):
            above_flux = flux[d - 1] if d else 0.0
            below_flux = lanes(flux[d], 16) if d < 7 else 0.0
            ret2[d] = jnp.where(block == 0, above_flux, jnp.where(block == 1, below_flux, 0.0))
        ret2_rx[mine] = ret2[s]
        start(ret2_copies)

        top = jnp.zeros((8, 128), F32)
        bot = jnp.zeros((8, 128), F32)
        for j in range(7):
            top = jnp.where(block == j + 1, lanes(flux[j], 16 * (j + 1)), top)
            bot = jnp.where(block == j, lanes(flux[j], 16 * j), bot)
        x = jnp.stack([p[i] + e_up[i] * top - e_down[i] * bot for i in range(8)])
        diff = x[:-1] - x[1:]
        result = jnp.sum(wets[1:] * diff * lanes(diff, -8), axis=0)
        for shift in (64, 32, 16):
            result = result + lanes(result, shift)
        for j in range(7):
            jump = jnp.where(m_all[j] > 0.0, flux[j] / m_all[j], 0.0)
            result = result + jump * lanes(jump, -8)
        result = result + lanes(result, -2)
        result = -(result + lanes(result, -4))
        edge_bg[...] = jnp.where(first, result, lanes(result, 126))

    wet_back = wet * back
    b_east = jnp.where(last, 0.0, lanes(wet_back, 127))
    b_west = jnp.where(first, 0.0, lanes(wet_back, 1))
    b_north = to_north(wet_back)
    b_south = to_south(wet_back)
    grad = centre * wet_back + spread * (b_east + b_west + b_north + b_south)
    flow = shift_e[2] * b_east[:2] - shift_w[2] * b_west[:2] + m_north[3] * b_north[:2] - m_south[3] * b_south[:2]
    grad_t = grad[:2] + ADVECT * wet * flow
    grad_u = grad[2] - ADVECT * jnp.sum(wet_back[:2] * grad_x, axis=0) - latitude * wet_back[3]
    grad_v = grad[3] - ADVECT * jnp.sum(wet_back[:2] * grad_y, axis=0) + latitude * wet_back[2]

    arrived(far_copies[2:])
    from_west, from_east = halo_rx[0], halo_rx[1]
    cols = jnp.where(even, from_east[1], from_west[1])
    cols = jnp.stack([lanes(cols, -16 * i) for i in range(8)])
    depths = jnp.where(even, column(from_east[0], 0), column(from_west[0], 127))
    backs = jnp.where(even, column(from_east[0], 64), column(from_west[0], 63))
    _, h_wet, (h_sys, h_up, h_down) = edge_system(cols, jnp.full((8, 128), base), depths, backs)
    p_halo = local_solve(h_sys, [cols[i] for i in range(8)])
    m_halo = jnp.stack([lanes(cols, 127 - 2 * f) for f in range(4)])
    depth_halo = jnp.where(last, column(from_east[0], 0), column(from_west[0], 127))
    edge_wet = jnp.where(jnp.logical_and(edge, level < depth_halo), wet, 0.0)
    sign = jnp.where(last, ADVECT, jnp.where(first, -ADVECT, 0.0))
    m_edge = jnp.where(edge, m_halo, 0.0)
    delta = spread * m_edge - DIFFUSE * edge_wet * masked
    delta_t = delta[:2] - sign * zonal * m_edge[:2]
    delta = inter + jnp.concatenate([delta_t, delta[2:]], axis=0)
    p_after = local_solve(system, [delta[:, i] for i in range(8)])
    grad_t = grad_t - DIFFUSE * edge_wet * wet_back[:2]
    grad_u = grad_u - DIFFUSE * edge_wet * wet_back[2] - sign * jnp.sum(wet_back[:2] * m_edge[:2], axis=0)
    grad_v = grad_v - DIFFUSE * edge_wet * wet_back[3]

    for k, to in enumerate((0, end)):

        @pl.when(s != to)
        def _():
            send(ret2.at[0], ret2_rx.at[k], ret2_s.at[0], ret2_r.at[k], {"store": to}).wait_recv()

    west_edge, east_edge = ret2_rx[0], ret2_rx[1]
    own = jnp.where(even, west_edge, lanes(east_edge, -2))
    top_a = jnp.where(edge, jnp.stack([lanes(own, -2 * f) for f in range(4)]), top_a)
    bot_a = jnp.where(edge, jnp.stack([lanes(own, -2 * f - 16) for f in range(4)]), bot_a)
    coef, coef_top, coef_bot = coefficients(finish(p_after, top_a, bot_a), top_a, bot_a)
    slope = MIXING * coef * gate * (1.0 - gate)
    slope_top = MIXING * coef_top * gate_top * (1.0 - gate_top)
    slope_bot = MIXING * coef_bot * gate_bot * (1.0 - gate_bot)
    dens_grad = jnp.concatenate([slope, slope_bot[None]], axis=0) - jnp.concatenate([slope_top[None], slope], axis=0)

    h_flux = jnp.where(even, east_edge, west_edge)
    h_bot = lanes(h_flux, -16)
    h_back = h_wet * jnp.stack([p_halo[i] + h_up[i] * h_flux - h_down[i] * h_bot for i in range(8)])
    b_edge = jnp.where(edge, jnp.stack([lanes(h_back, 119 - 2 * f) for f in range(4)]), 0.0)
    flow = sign * m_edge[2]
    add = spread * b_edge
    out[0] = grad_t[0] + add[0] + wet * (flow * b_edge[0] - ALPHA_T * dens_grad)
    out[1] = grad_t[1] + add[1] + wet * (flow * b_edge[1] + BETA_S * dens_grad)
    out[2] = grad_u + add[2]
    out[3] = grad_v + add[3]

    arrived(part_copies)
    bg_out[...] = jnp.sum(part_rx[...], axis=0)

    @pl.when(owner)
    def _():
        bg_out[...] = jnp.where(edge, edge_bg[...], bg_out[...])
        for copy in ret2_copies:
            copy.wait_send()

    for to, copy in own_copies:
        pl.when(s != to)(copy.wait_send)
    for copies in (far_copies, early_copies, dens_copies, ret1_copies, part_copies):
        for copy in copies:
            copy.wait_send()


def shards(n_tile, n_store, state, cotangent, land_mask, wet_count, background):
    tile = (8, 128)
    vmem = functools.partial(pltpu.VMEM, dtype=F32)
    sem = pltpu.SemaphoreType.DMA
    n, mates = n_store, n_store - 1
    grad, bg_sum = pl.pallas_call(
        functools.partial(kernel, n_tile, n_store),
        name="ocean",
        out_shape=(jax.ShapeDtypeStruct(state.shape, F32), jax.ShapeDtypeStruct(tile, F32)),
        in_specs=[pl.BlockSpec(memory_space=pl.ANY)] * 5,
        out_specs=(pl.BlockSpec(memory_space=pltpu.VMEM), pl.BlockSpec(memory_space=pltpu.VMEM)),
        scratch_shapes=[
            vmem(state.shape), vmem(state.shape),
            pltpu.VMEM(tile, jnp.int32), pltpu.VMEM(tile, jnp.int32), vmem(tile),
            vmem((2,) + tile), vmem((2,) + tile), vmem((2, 2) + tile), vmem((n, 2) + tile), vmem((n, 2) + tile),
            vmem((2,) + tile), vmem((2,) + tile),
            vmem((n, 3) + tile), vmem((n, 3) + tile),
            vmem((n, 2) + tile), vmem((n, 2) + tile),
            vmem((n,) + tile), vmem((2,) + tile),
            vmem(tile), vmem((n,) + tile), vmem(tile),
            sem((5,)), sem((2,)), sem((2,)), sem((2,)), sem((n,)), sem((2,)), sem((n,)), sem((2,)), sem((2,)),
            sem((mates,)), sem((mates,)), sem((mates,)), sem((mates,)), sem((mates,)), sem((2,)),
            sem((mates,)), sem((mates,)), pltpu.SemaphoreType.REGULAR, pltpu.SemaphoreType.REGULAR,
        ],
        compiler_params=pltpu.CompilerParams(collective_id=0, has_side_effects=True),
    )(state, cotangent, land_mask, wet_count, background)
    part = state.shape[3] // n_store
    return grad, lax.dynamic_slice_in_dim(bg_sum, lax.axis_index("store") * part, part, 1)


def solution(mesh):
    in_specs = (
        P(None, "store", None, "tile"),
        P(None, "store", None, "tile"),
        P(None, "tile"),
        P(None, "tile"),
        P(None, "tile"),
    )
    out_specs = (P(None, "store", None, "tile"), P(None, ("tile", "store")))
    body = functools.partial(shards, mesh.shape["tile"], mesh.shape["store"])
    return jax.shard_map(body, mesh=mesh, in_specs=in_specs, out_specs=out_specs, check_vma=False)
```

time: 34.5 us -> 27.8 us (0.81)
  Pallas kernels: 30.8 us -> 24 us
    pallas_call x1, Pallas kernels: 30.8 us -> 24 us  [shards(): pl.pallas_call(functools.partial(kernel, n_tile, n_store), name='ocean',...]
where the time goes in v3:
time: 27.8 us; the launch traced here: 27.6 us
  Pallas kernels  24 us (86%)
  local copies, waits for them, and re-layouts  2.92 us (11%)
  between operations  0.64 us (2%)
    pallas_call x1, Pallas kernels, shards(): pl.pallas_call(functools.partial(kernel, n_tile, n_store), name='ocean',...  24 us
    unnamed x1, local copies, waits for them, and re-layouts  1.57 us
    dynamic_slice x1, local copies, waits for them, and re-layouts, shards(): lax.dynamic_slice_in_dim(bg_sum, lax.axis_index('store') * part, part, 1)  1.36 us

profile of v3, /device:TPU:1, one launch (start us, length us, event | category | flops | bytes accessed | tf_op | source)
XLA Modules:
  0.0 27.6 jit_solution(3298644540302780983)
XLA Ops:
  0.6 24.0 %ocean.1 = (f32[4,8,8,128]{3,2,1,0:T(8,128)}, f32[8,128]{1,0:T(8,128)}) custom-call(f32[4,8,8,128]{3,2,1,0:T(8,128)} %state_h.1, f32[4,8,8,128]{3,2,1,0:T(8,128)} %cot_h.1, s32[8,128]{1,0:T(8,128)} %land_h.1, s32[8,128]{1,0:T(8,128)} %count_h.1, f32[8,128]{1,0:T(8,128)} %bg_h.1), custom_call_target="tpu_custom_call" | custom-call | tf_op jit(solution)/shard_map/ocean/pallas_call | solution.py:496
  24.7 1.4 %constant_dynamic-slice_fusion = f32[8,16]{1,0:T(8,128)} fusion(f32[8,128]{1,0:T(8,128)} %get-tuple-element.5, s32[]{:T(128)S(6)} %select_n.3), kind=kLoop, calls=%fused_computation | loop fusion | bytes 1028 | tf_op jit(solution)/shard_map/dynamic_slice | solution.py:518
  26.0 1.6 %copy.8 = f32[4,8,8,128]{3,2,1,0:T(8,128)} copy(f32[4,8,8,128]{3,2,1,0:T(8,128)} %get-tuple-element.8) | data formatting | bytes 262144

commit v4 on v3

--- a/solution.py
+++ b/solution.py
@@ -445,6 +445,13 @@
     grad_u = grad_u - DIFFUSE * edge_wet * wet_back[2] - sign * jnp.sum(wet_back[:2] * m_edge[:2], axis=0)
     grad_v = grad_v - DIFFUSE * edge_wet * wet_back[3]
 
+    arrived(part_copies)
+    bg_out[...] = jnp.sum(part_rx[...], axis=0)
+
+    @pl.when(owner)
+    def _():
+        bg_out[...] = jnp.where(edge, edge_bg[...], bg_out[...])
+
     for k, to in enumerate((0, end)):
 
         @pl.when(s != to)
@@ -472,12 +479,8 @@
     out[2] = grad_u + add[2]
     out[3] = grad_v + add[3]
 
-    arrived(part_copies)
-    bg_out[...] = jnp.sum(part_rx[...], axis=0)
-
     @pl.when(owner)
     def _():
-        bg_out[...] = jnp.where(edge, edge_bg[...], bg_out[...])
         for copy in ret2_copies:
             copy.wait_send()
 
@@ -497,7 +500,7 @@
         functools.partial(kernel, n_tile, n_store),
         name="ocean",
         out_shape=(jax.ShapeDtypeStruct(state.shape, F32), jax.ShapeDtypeStruct(tile, F32)),
-        in_specs=[pl.BlockSpec(memory_space=pl.ANY)] * 5,
+        in_specs=[pl.BlockSpec(memory_space=pltpu.HBM)] * 5,
         out_specs=(pl.BlockSpec(memory_space=pltpu.VMEM), pl.BlockSpec(memory_space=pltpu.VMEM)),
         scratch_shapes=[
             vmem(state.shape), vmem(state.shape),
@@ -512,8 +515,8 @@
             sem((mates,)), sem((mates,)), sem((mates,)), sem((mates,)), sem((mates,)), sem((2,)),
             sem((mates,)), sem((mates,)), pltpu.SemaphoreType.REGULAR, pltpu.SemaphoreType.REGULAR,
         ],
-        compiler_params=pltpu.CompilerParams(collective_id=0, has_side_effects=True),
-    )(state, cotangent, land_mask, wet_count, background)
+        compiler_params=pltpu.CompilerParams(collective_id=0, has_side_effects=True, vmem_limit_bytes=8 << 20),
+    )(*[pltpu.with_memory_space_constraint(x, pltpu.HBM) for x in (state, cotangent, land_mask, wet_count, background)])
     part = state.shape[3] // n_store
     return grad, lax.dynamic_slice_in_dim(bg_sum, lax.axis_index("store") * part, part, 1)
 

time: 27.8 us -> 25.4 us (0.914)
  local copies, waits for them, and re-layouts: 2.92 us -> 1.33 us
  Pallas kernels: 24 us -> 23.4 us
    unnamed x1, local copies, waits for them, and re-layouts: 1.57 us -> 0.65 us
    dynamic_slice x1, local copies, waits for them, and re-layouts: 1.36 us -> 0.67 us  [shards(): lax.dynamic_slice_in_dim(bg_sum, lax.axis_index('store') * part, part, 1)]
    pallas_call x1, Pallas kernels: 24 us -> 23.4 us  [shards(): pl.pallas_call(functools.partial(kernel, n_tile, n_store), name='ocean',...]
where the time goes in v4:
time: 25.4 us; the launch traced here: 25.3 us
  Pallas kernels  23.4 us (92%)
  local copies, waits for them, and re-layouts  1.33 us (5%)
  between operations  0.64 us (3%)
    pallas_call x1, Pallas kernels, shards(): pl.pallas_call(functools.partial(kernel, n_tile, n_store), name='ocean',...  23.4 us
    dynamic_slice x1, local copies, waits for them, and re-layouts, shards(): lax.dynamic_slice_in_dim(bg_sum, lax.axis_index('store') * part, part, 1)  0.67 us
    unnamed x1, local copies, waits for them, and re-layouts  0.65 us

profile of v4, /device:TPU:1, one launch (start us, length us, event | category | flops | bytes accessed | tf_op | source)
XLA Modules:
  0.0 25.3 jit_solution(7855417650084991010)
XLA Ops:
  0.6 23.4 %ocean.1 = (f32[4,8,8,128]{3,2,1,0:T(8,128)S(1)}, f32[8,128]{1,0:T(8,128)S(1)}) custom-call(f32[4,8,8,128]{3,2,1,0:T(8,128)} %state_h.1, f32[4,8,8,128]{3,2,1,0:T(8,128)} %cot_h.1, s32[8,128]{1,0:T(8,128)} %land_h.1, s32[8,128]{1,0:T(8,128)} %count_h.1, f32[8,128]{1,0:T(8,128)} %bg_h.1), custom_call_target="tpu_custom_call" | custom-call | tf_op jit(solution)/shard_map/ocean/pallas_call | solution.py:499
  24.0 0.7 %constant_dynamic-slice_fusion = f32[8,16]{1,0:T(8,128)} fusion(f32[8,128]{1,0:T(8,128)S(1)} %get-tuple-element.5, s32[]{:T(128)S(6)} %select_n.3), kind=kLoop, calls=%fused_computation | loop fusion | bytes 1028 | tf_op jit(solution)/shard_map/dynamic_slice | solution.py:521
  24.7 0.7 %copy.8 = f32[4,8,8,128]{3,2,1,0:T(8,128)} copy(f32[4,8,8,128]{3,2,1,0:T(8,128)S(1)} %get-tuple-element.8) | data formatting | bytes 262144

commit v5 on v3

v5 whole, which is shorter than its diff:
```python
import functools

import jax
import jax.numpy as jnp
from jax import lax
from jax.experimental import pallas as pl
from jax.experimental.pallas import tpu as pltpu
from jax.sharding import PartitionSpec as P

DIFFUSE = 0.1
ADVECT = 0.05
MIXING = 2.0
ALPHA_T = 0.6
BETA_S = 0.8
MESH = pl.DeviceIdType.MESH
F32 = jnp.float32


def lanes(x, shift):
    shift %= 128
    return pltpu.roll(x, shift, x.ndim - 1) if shift else x


def rows(x, shift):
    return pltpu.roll(x, shift % 8, x.ndim - 2)


def kernel(
    n_tile, n_store, state_h, cot_h, land_h, count_h, bg_h, out, bg_out,
    st, ct, land, count, bg,
    xa, xb, halo_rx, own_rx, dens_tx, dens_rx,
    early, early_rx, ret1, ret1_rx, part, part_rx, back_tx, back_rx,
    in_sem, halo_s, halo_r, own_s, own_r, dens_s, dens_r,
    early_s, early_r, ret1_s, ret1_r, part_s, part_r, back_s, back_r, near, far,
):
    t = lax.axis_index("tile")
    s = lax.axis_index("store")
    east = lax.rem(t + 1, n_tile)
    west = lax.rem(t + n_tile - 1, n_tile)
    below = lax.rem(s + 1, n_store)
    above = lax.rem(s + n_store - 1, n_store)
    end = n_store - 1
    owner = jnp.logical_or(s == 0, s == end)
    late = lax.rem(t // 4, 2) == 1

    barrier = pltpu.get_barrier_semaphore()

    def greet(**where):
        pl.semaphore_signal(barrier, inc=1, device_id=where, device_id_type=MESH)

    core = lax.rem(s, 2)
    chip = s - core
    other = {"store": chip + 1 - core}
    for to in (east, west):
        for d in range(1, n_store, 2):
            greet(tile=to, store=d)
    greet(**other)
    for d in range(2, n_store, 2):
        greet(store=lax.rem(chip + d, n_store))

    loads = [
        pltpu.make_async_copy(src, dst, in_sem.at[i])
        for i, (src, dst) in enumerate(((land_h, land), (count_h, count), (bg_h, bg), (state_h, st), (cot_h, ct)))
    ]
    for load in loads:
        load.start()

    lane = lax.broadcasted_iota(jnp.int32, (8, 128), 1)
    row = lax.broadcasted_iota(jnp.int32, (8, 128), 0)
    block = lane >> 4
    field = (lane & 15) >> 1
    even = (lane & 1) == 0
    pairs = ((lane + 1) & 127) >> 1
    first = lane == 0
    last = lane == 127
    edge = jnp.logical_or(first, last)

    def send(src, dst, send_sem, recv_sem, where):
        return pltpu.make_async_remote_copy(
            src_ref=src, dst_ref=dst, send_sem=send_sem, recv_sem=recv_sem, device_id=where, device_id_type=MESH
        )

    def mates(src, dst, send_sem, recv_sem):
        copies = []
        for d in range(1, n_store):
            to = lax.rem(s + d, n_store)
            copies.append(send(src(to), dst.at[s], send_sem.at[d - 1], recv_sem.at[d - 1], {"store": to}))
        return copies

    def start(copies):
        for copy in copies:
            copy.start()

    def arrived(copies):
        for copy in copies:
            copy.wait_recv()

    def exchange_blocks(tiles):
        tiles = list(tiles)
        for b in (4, 2, 1):
            keep = (block & b) == 0
            new = [None] * 8
            for v in range(8):
                if v & b == 0:
                    lo, hi = tiles[v], tiles[v + b]
                    new[v] = jnp.where(keep, lo, lanes(hi, 16 * b))
                    new[v + b] = jnp.where(keep, lanes(lo, -16 * b), hi)
            tiles = new
        return tiles

    def pack_edges(tiles, bits):
        for bit in bits:
            half = tiles.shape[0] // 2
            tiles = jnp.where((pairs & bit) != 0, lanes(tiles[half:], 2 * bit), tiles[:half])
        return tiles[0]

    def beside(x):
        return jnp.where(even, x, lanes(x, 2))

    def column(x, c):
        return jnp.broadcast_to(x[:, c : c + 1], (8, 128))

    def to_north(x):
        return jnp.where(row == 7, 0.0, rows(x, 7))

    def to_south(x):
        return jnp.where(row == 0, 0.0, rows(x, 1))

    def eliminate(mix):
        ratio, inverse = [], []
        excess = jnp.ones((8, 128), F32)
        for i in range(7):
            inv = 1.0 / (excess + mix[i])
            ratio.append(mix[i] * inv)
            inverse.append(inv)
            excess = 1.0 + ratio[i] * excess
        inverse.append(1.0 / excess)
        up = [inverse[0]]
        for i in range(1, 8):
            up.append(mix[i - 1] * up[-1] * inverse[i])
        for i in range(6, -1, -1):
            up[i] = up[i] + ratio[i] * up[i + 1]
        down = [None] * 7 + [inverse[7]]
        for i in range(6, -1, -1):
            down[i] = ratio[i] * down[i + 1]
        return (mix, ratio, inverse), up, down

    def local_solve(system, rhs):
        mix, ratio, inverse = system
        values = [rhs[0] * inverse[0]]
        for i in range(1, 8):
            values.append((rhs[i] + mix[i - 1] * values[-1]) * inverse[i])
        for i in range(6, -1, -1):
            values[i] = values[i] + ratio[i] * values[i + 1]
        return values

    def edge_density(tiles):
        dens = -ALPHA_T * tiles + BETA_S * lanes(tiles, -2)
        for bit in (1, 2, 4):
            dens = jnp.where((field & bit) == 0, dens, lanes(dens, 2 * bit))
        return dens

    def sides(a, b):
        return jnp.where(even, a, b)

    def reduce_blocks(tiles):
        m_inv, low, high = [], [], []
        for j in range(7):
            here, there = tiles[j], tiles[j + 1]
            weight = lanes(here, -80)
            gates = jax.nn.sigmoid(lanes(here, -64) - lanes(there, -48))
            m = jnp.where(weight > 0.0, weight + MIXING * gates, 0.0)
            pivot = 1.0 + m * (lanes(here, -32) + there)
            lower = m * lanes(here, -16)
            if j:
                pivot = pivot - lower * high[-1]
            inv = 1.0 / jnp.where(block == 0, pivot, 1.0)
            m_inv.append(m * inv)
            low.append(lower * inv)
            high.append(m * lanes(there, -16) * inv)
        return m_inv, low, high

    def fluxes(m_inv, low, high, jumps):
        flux = []
        for j in range(7):
            value = m_inv[j] * jumps[j]
            flux.append(value + low[j] * flux[-1] if j else value)
        for j in range(5, -1, -1):
            flux[j] = flux[j] + high[j] * flux[j + 1]
        return flux

    level = (lax.broadcasted_iota(jnp.int32, (8, 8, 128), 0) + s * 8).astype(F32)
    base = (s * 8).astype(F32)

    for load in loads:
        load.wait()
    depth = jnp.where(land[...] == 1, count[...], 0).astype(F32)
    wet = jnp.where(level < depth, 1.0, 0.0)
    backgr = bg[...]
    masked = st[...] * wet
    fields = [masked[f] for f in range(4)] + [ct[f] for f in range(4)]
    packed = pack_edges(jnp.stack([fields[f][i] for i in range(8) for f in range(8)]), (32, 16, 8, 4, 2, 1))
    own_edges = beside(packed)

    def extra(c):
        return jnp.where(field == 0, column(depth, c), column(backgr, c))

    xa[0] = sides(extra(127), own_edges)
    xa[1] = sides(own_edges, extra(0))
    xb[0] = own_edges
    far_copies = []
    for side, to in enumerate((east, west)):
        for d in range(n_store):
            far_copies.append(
                send(xa.at[side], halo_rx.at[side, s], halo_s.at[side, d], halo_r.at[side, s], {"tile": to, "store": d})
            )

    def to_neighbours():
        @pl.when(core == 1)
        def _():
            pl.semaphore_wait(barrier, 2 * n_store + 1)
            pl.semaphore_signal(far, inc=1, device_id=other, device_id_type=MESH)

        @pl.when(core == 0)
        def _():
            pl.semaphore_wait(far, 1)

        start(far_copies)

    pl.when(late)(to_neighbours)

    density = -ALPHA_T * masked[0] + BETA_S * masked[1]
    dens_tx[0] = density[7]
    dens_tx[1] = density[0]
    gate = jax.nn.sigmoid(density[:-1] - density[1:])
    pair = wet[1:]
    system, up, down = eliminate((backgr + MIXING * gate) * pair)
    p_back = local_solve(system, [ct[:, i] for i in range(8)])

    shift_e = jnp.where(last, 0.0, lanes(masked, 127))
    shift_w = jnp.where(first, 0.0, lanes(masked, 1))
    around = jnp.where(level < jnp.where(last, 0.0, lanes(depth, 127)), 1.0, 0.0)
    around += jnp.where(level < jnp.where(first, 0.0, lanes(depth, 1)), 1.0, 0.0)
    around += jnp.where(level < to_north(depth), 1.0, 0.0)
    around += jnp.where(level < to_south(depth), 1.0, 0.0)
    centre = wet * (1.0 - DIFFUSE * around)
    spread = DIFFUSE * wet
    m_north = to_north(masked)
    m_south = to_south(masked)
    latitude = 0.1 + 0.2 * (row.astype(F32) + 0.5) / 8.0
    inter = centre * masked + spread * (shift_e + shift_w + m_north + m_south)
    zonal, merid = masked[2], masked[3]
    grad_x = shift_e[:2] - shift_w[:2]
    grad_y = m_north[:2] - m_south[:2]
    advect = -ADVECT * (zonal * grad_x + merid * grad_y)
    inter = [inter[0] + advect[0], inter[1] + advect[1], inter[2] + latitude * merid, inter[3] - latitude * zonal]
    xb[1] = beside(pack_edges(jnp.stack([inter[f][i] for i in range(8) for f in range(4)]), (32, 16, 8, 2, 1)))
    inter = jnp.stack(inter)
    p_after = local_solve(system, [inter[:, i] for i in range(8)])

    bottom_wet = base + 8.0 < depth
    bg_pair = jnp.where(bottom_wet, backgr, 0.0)
    groups = (
        [p_back[0][f] for f in range(4)] + [p_back[7][f] for f in range(4)],
        [p_after[0][f] for f in range(4)] + [p_after[7][f] for f in range(4)],
        [up[0], up[7], down[7], density[0], density[7], bg_pair, bg_pair, bg_pair],
    )
    for g, group in enumerate(groups):
        for d, tile in enumerate(exchange_blocks(group)):
            early[d, g] = tile
    early_rx[s] = early[s]
    own_rx[s] = xb[...]

    @pl.when(core == 0)
    def _():
        pl.semaphore_wait(barrier, end)
        pl.semaphore_signal(near, inc=1, device_id=other, device_id_type=MESH)

    @pl.when(core == 1)
    def _():
        pl.semaphore_wait(near, 1)

    early_copies = mates(lambda to: early.at[to], early_rx, early_s, early_r)
    start(early_copies)
    dens_copies = [
        send(dens_tx.at[0], dens_rx.at[0], dens_s.at[0], dens_r.at[0], {"store": below}),
        send(dens_tx.at[1], dens_rx.at[1], dens_s.at[1], dens_r.at[1], {"store": above}),
    ]
    start(dens_copies)
    own_copies = mates(lambda to: xb, own_rx, own_s, own_r)
    start(own_copies)

    arrived(early_copies)
    coefs = reduce_blocks([early_rx[j, 2] for j in range(8)])

    def four(x):
        x = jnp.where(block == 0, x, lanes(x, 16))
        return jnp.where(block < 2, x, lanes(x, 32))

    coefs = [[four(x) for x in xs] for xs in coefs]
    left = lane < 64
    for g in range(2):
        ends = [early_rx[j, g] for j in range(8)]
        flux = fluxes(*coefs, [lanes(ends[j], 64) - ends[j + 1] for j in range(7)])
        for d in range(8):
            above_flux = flux[d - 1] if d else 0.0
            below_flux = lanes(flux[d], 64) if d < 7 else 0.0
            ret1[d, g] = jnp.where(left, above_flux, below_flux)
    ret1_rx[s] = ret1[s]
    ret1_copies = mates(lambda to: ret1.at[to], ret1_rx, ret1_s, ret1_r)
    start(ret1_copies)
    pl.when(jnp.logical_not(late))(to_neighbours)

    arrived(dens_copies)
    gate_top = jax.nn.sigmoid(dens_rx[0] - density[0])
    gate_bot = jax.nn.sigmoid(density[7] - dens_rx[1])
    pair_top = jnp.where(base > 0.0, wet[0], 0.0)
    pair_bot = jnp.where(bottom_wet, 1.0, 0.0)
    scale_top = pair_top / (backgr + MIXING * gate_top)
    scale_bot = pair_bot / (backgr + MIXING * gate_bot)

    def coefficients(after, top_a, bot_a):
        coef = -jnp.sum(diff_b * (after[:, :-1] - after[:, 1:]), axis=0) * pair
        coef_top = -jnp.sum(top_b * top_a, axis=0) * (scale_top * scale_top)
        coef_bot = -jnp.sum(bot_b * bot_a, axis=0) * (scale_bot * scale_bot)
        return coef, coef_top, coef_bot

    def finish(p, top, bot):
        return jnp.stack([p[i] + up[i] * top - down[i] * bot for i in range(8)], axis=1)

    arrived(ret1_copies)
    flux_b = exchange_blocks([ret1_rx[d, 0] for d in range(8)])
    flux_a = exchange_blocks([ret1_rx[d, 1] for d in range(8)])
    top_b, bot_b = jnp.stack(flux_b[:4]), jnp.stack(flux_b[4:])
    top_a, bot_a = jnp.stack(flux_a[:4]), jnp.stack(flux_a[4:])
    back = finish(p_back, top_b, bot_b)
    diff_b = back[:, :-1] - back[:, 1:]
    after = finish(p_after, top_a, bot_a)
    coef, _, coef_bot = coefficients(after, top_a, bot_a)
    total = jnp.sum(coef, axis=0) + coef_bot
    part[...] = total
    part_rx[s] = total
    part_copies = mates(lambda to: part, part_rx, part_s, part_r)
    start(part_copies)
    wet_back = wet * back
    back_tx[...] = beside(pack_edges(jnp.stack([back[f, i] for i in range(8) for f in range(4)]), (32, 16, 8, 2, 1)))
    back_rx[s] = back_tx[...]
    back_copies = [
        (to, send(back_tx, back_rx.at[s], back_s.at[k], back_r.at[s], {"store": to})) for k, to in enumerate((0, end))
    ]
    for to, copy in back_copies:
        pl.when(s != to)(copy.start)


    b_east = jnp.where(last, 0.0, lanes(wet_back, 127))
    b_west = jnp.where(first, 0.0, lanes(wet_back, 1))
    b_north = to_north(wet_back)
    b_south = to_south(wet_back)
    grad = centre * wet_back + spread * (b_east + b_west + b_north + b_south)
    flow = shift_e[2] * b_east[:2] - shift_w[2] * b_west[:2] + m_north[3] * b_north[:2] - m_south[3] * b_south[:2]
    grad_t = grad[:2] + ADVECT * wet * flow
    grad_u = grad[2] - ADVECT * jnp.sum(wet_back[:2] * grad_x, axis=0) - latitude * wet_back[3]
    grad_v = grad[3] - ADVECT * jnp.sum(wet_back[:2] * grad_y, axis=0) + latitude * wet_back[2]

    arrived(own_copies)
    own = jnp.stack(exchange_blocks([own_rx[j, 0] for j in range(8)]))
    own_inter = jnp.stack(exchange_blocks([own_rx[j, 1] for j in range(8)]))
    own_dens = edge_density(own)
    start_level = (block * 8).astype(F32)
    edge_level = jnp.stack([start_level + i for i in range(8)])
    own_depth = sides(column(depth, 0), column(depth, 127))
    own_bg = sides(column(backgr, 0), column(backgr, 127))
    along = jnp.where(field == 0, lanes(own, -4), lanes(own, -2)) * sides(ADVECT, -ADVECT)
    along = jnp.where(field < 2, along, 0.0)
    own_wet = jnp.where(edge_level < own_depth, DIFFUSE, 0.0)

    for side in range(2):
        for src in range(n_store):
            send(xa.at[0], halo_rx.at[side, src], halo_s.at[0, 0], halo_r.at[side, src], {"tile": east}).wait_recv()
    halo = jnp.stack(exchange_blocks([sides(halo_rx[1, j], halo_rx[0, j]) for j in range(8)]))
    from_west, from_east = halo_rx[0, 0], halo_rx[1, 0]
    west_depth, east_depth = column(from_west, 0), column(from_east, 1)
    inner = field < 4
    dens = jnp.where(inner, own_dens, edge_density(halo))
    depths = jnp.where(inner, own_depth, sides(east_depth, west_depth))
    backs = jnp.where(inner, own_bg, sides(column(from_east, 3), column(from_west, 2)))
    edge_wet = jnp.where(edge_level < depths, 1.0, 0.0)
    halo_wet = jnp.where(edge_level < sides(west_depth, east_depth), 1.0, 0.0)
    swapped = sides(lanes(halo, -1), lanes(halo, 1))
    delta = own_wet * (swapped - halo_wet * own) + along * swapped
    rhs = jnp.where(inner, own_inter + delta, halo)
    edge_sys, e_up, e_down = eliminate((backs + MIXING * jax.nn.sigmoid(dens[:-1] - dens[1:])) * edge_wet[1:])
    p = local_solve(edge_sys, [rhs[i] for i in range(8)])
    weight = jnp.where(start_level + 8.0 < depths, backs, 0.0)
    blocks = exchange_blocks([e_up[0], e_up[7], e_down[7], dens[0], dens[7], weight, p[0], p[7]])
    jumps = [lanes(blocks[j], -112) - lanes(blocks[j + 1], -96) for j in range(7)]
    flux = fluxes(*reduce_blocks(blocks), jumps)
    bot = jnp.where(block == 0, flux[0], 0.0)
    for j in range(1, 7):
        bot = jnp.where(block == j, lanes(flux[j], 16 * j), bot)
    top = lanes(bot, 16)
    solved = jnp.stack([p[i] + e_up[i] * top - e_down[i] * bot for i in range(8)])

    here = jnp.concatenate([solved, top[None], bot[None]], axis=0)
    for bit in (1, 2, 4):
        here = jnp.where((s & bit) != 0, lanes(here, -16 * bit), here)
    own_here = sides(here, lanes(here, -2))
    own_here = jnp.stack([lanes(own_here, -2 * f) for f in range(4)])
    after = jnp.where(edge, own_here[:, :8], after)
    top_a = jnp.where(edge, own_here[:, 8], top_a)
    bot_a = jnp.where(edge, own_here[:, 9], bot_a)
    b_edge = jnp.stack([lanes(here[:8], 119 - 2 * f) for f in range(4)])
    cols = sides(halo_rx[1, s], halo_rx[0, s])
    cols = jnp.stack([lanes(cols, -16 * i) for i in range(8)])
    m_edge = jnp.stack([lanes(cols, 127 - 2 * f) for f in range(3)])
    beside_wet = jnp.where(jnp.logical_and(edge, level < jnp.where(last, east_depth, west_depth)), DIFFUSE * wet, 0.0)
    edge_flow = jnp.where(edge, b_edge * beside_wet, 0.0) - beside_wet * wet_back
    sign = jnp.where(last, ADVECT, jnp.where(first, -ADVECT, 0.0))
    flow = jnp.where(edge, sign * m_edge[2] * jnp.where(beside_wet > 0.0, 1.0, 0.0), 0.0)
    coef, coef_top, coef_bot = coefficients(after, top_a, bot_a)
    slope = MIXING * coef * gate * (1.0 - gate)
    slope_top = MIXING * coef_top * gate_top * (1.0 - gate_top)
    slope_bot = MIXING * coef_bot * gate_bot * (1.0 - gate_bot)
    dens_grad = wet * (
        jnp.concatenate([slope, slope_bot[None]], axis=0) - jnp.concatenate([slope_top[None], slope], axis=0)
    )
    pull = jnp.where(edge, sign * jnp.sum(wet_back[:2] * m_edge[:2], axis=0), 0.0)
    out[0] = grad_t[0] + edge_flow[0] + flow * b_edge[0] - ALPHA_T * dens_grad
    out[1] = grad_t[1] + edge_flow[1] + flow * b_edge[1] + BETA_S * dens_grad
    out[2] = grad_u + edge_flow[2] - pull
    out[3] = grad_v + edge_flow[3]

    arrived(part_copies)
    bg_out[...] = jnp.sum(part_rx[...], axis=0)

    @pl.when(owner)
    def _():
        for d in range(1, n_store):
            src = lax.rem(s + d, n_store)
            send(back_tx, back_rx.at[src], back_s.at[0], back_r.at[src], {"store": src}).wait_recv()
        own_back = jnp.stack(exchange_blocks([back_rx[j] for j in range(8)]))
        result = jnp.sum(edge_wet[1:] * (solved[:-1] - solved[1:]) * (own_back[:-1] - own_back[1:]), axis=0)
        jump = (solved[7] - lanes(solved[0], -16)) * (own_back[7] - lanes(own_back[0], -16))
        result = result + jnp.where(weight > 0.0, jump, 0.0)
        for shift in (64, 32, 16):
            result = result + lanes(result, shift)
        result = result + lanes(result, -2)
        result = -(result + lanes(result, -4))
        bg_out[...] = jnp.where(first, result, jnp.where(last, lanes(result, 126), bg_out[...]))

    for to, copy in back_copies:
        pl.when(s != to)(copy.wait_send)
    for copies in (far_copies, early_copies, dens_copies, own_copies, ret1_copies, part_copies):
        for copy in copies:
            copy.wait_send()


def shards(n_tile, n_store, state, cotangent, land_mask, wet_count, background):
    tile = (8, 128)
    vmem = functools.partial(pltpu.VMEM, dtype=F32)
    sem = pltpu.SemaphoreType.DMA
    n, mates = n_store, n_store - 1
    grad, bg_sum = pl.pallas_call(
        functools.partial(kernel, n_tile, n_store),
        name="ocean",
        out_shape=(jax.ShapeDtypeStruct(state.shape, F32), jax.ShapeDtypeStruct(tile, F32)),
        in_specs=[pl.BlockSpec(memory_space=pltpu.HBM)] * 5,
        out_specs=(pl.BlockSpec(memory_space=pltpu.VMEM), pl.BlockSpec(memory_space=pltpu.VMEM)),
        scratch_shapes=[
            vmem(state.shape), vmem(state.shape),
            pltpu.VMEM(tile, jnp.int32), pltpu.VMEM(tile, jnp.int32), vmem(tile),
            vmem((2,) + tile), vmem((2,) + tile), vmem((2, n) + tile), vmem((n, 2) + tile),
            vmem((2,) + tile), vmem((2,) + tile),
            vmem((n, 3) + tile), vmem((n, 3) + tile),
            vmem((n, 2) + tile), vmem((n, 2) + tile),
            vmem(tile), vmem((n,) + tile), vmem(tile), vmem((n,) + tile),
            sem((5,)), sem((2, n)), sem((2, n)), sem((mates,)), sem((mates,)), sem((2,)), sem((2,)),
            sem((mates,)), sem((mates,)), sem((mates,)), sem((mates,)), sem((mates,)), sem((mates,)),
            sem((2,)), sem((n,)), pltpu.SemaphoreType.REGULAR, pltpu.SemaphoreType.REGULAR,
        ],
        compiler_params=pltpu.CompilerParams(collective_id=0, has_side_effects=True, vmem_limit_bytes=8 << 20),
    )(*[pltpu.with_memory_space_constraint(x, pltpu.HBM) for x in (state, cotangent, land_mask, wet_count, background)])
    part = state.shape[3] // n_store
    return grad, lax.dynamic_slice_in_dim(bg_sum, lax.axis_index("store") * part, part, 1)


def solution(mesh):
    in_specs = (
        P(None, "store", None, "tile"),
        P(None, "store", None, "tile"),
        P(None, "tile"),
        P(None, "tile"),
        P(None, "tile"),
    )
    out_specs = (P(None, "store", None, "tile"), P(None, ("tile", "store")))
    body = functools.partial(shards, mesh.shape["tile"], mesh.shape["store"])
    return jax.shard_map(body, mesh=mesh, in_specs=in_specs, out_specs=out_specs, check_vma=False)
```

time: 27.8 us -> 22 us (0.79)
  Pallas kernels: 24 us -> 19.8 us
  local copies, waits for them, and re-layouts: 2.92 us -> 1.33 us
    pallas_call x1, Pallas kernels: 24 us -> 19.8 us  [shards(): pl.pallas_call(functools.partial(kernel, n_tile, n_store), name='ocean',...]
    unnamed x1, local copies, waits for them, and re-layouts: 1.57 us -> 0.65 us
    dynamic_slice x1, local copies, waits for them, and re-layouts: 1.36 us -> 0.67 us  [shards(): lax.dynamic_slice_in_dim(bg_sum, lax.axis_index('store') * part, part, 1)]
where the time goes in v5:
time: 22 us; the launch traced here: 21.8 us
  Pallas kernels  19.8 us (90%)
  local copies, waits for them, and re-layouts  1.33 us (6%)
  between operations  0.64 us (3%)
    pallas_call x1, Pallas kernels, shards(): pl.pallas_call(functools.partial(kernel, n_tile, n_store), name='ocean',...  19.8 us
    dynamic_slice x1, local copies, waits for them, and re-layouts, shards(): lax.dynamic_slice_in_dim(bg_sum, lax.axis_index('store') * part, part, 1)  0.67 us
    unnamed x1, local copies, waits for them, and re-layouts  0.65 us

profile of v5, /device:TPU:1, one launch (start us, length us, event | category | flops | bytes accessed | tf_op | source)
XLA Modules:
  0.0 21.8 jit_solution(16776779364800182151)
XLA Ops:
  0.6 19.8 %ocean.1 = (f32[4,8,8,128]{3,2,1,0:T(8,128)S(1)}, f32[8,128]{1,0:T(8,128)S(1)}) custom-call(f32[4,8,8,128]{3,2,1,0:T(8,128)} %state_h.1, f32[4,8,8,128]{3,2,1,0:T(8,128)} %cot_h.1, s32[8,128]{1,0:T(8,128)} %land_h.1, s32[8,128]{1,0:T(8,128)} %count_h.1, f32[8,128]{1,0:T(8,128)} %bg_h.1), custom_call_target="tpu_custom_call" | custom-call | tf_op jit(solution)/shard_map/ocean/pallas_call | solution.py:463
  20.4 0.7 %constant_dynamic-slice_fusion = f32[8,16]{1,0:T(8,128)} fusion(f32[8,128]{1,0:T(8,128)S(1)} %get-tuple-element.5, s32[]{:T(128)S(6)} %select_n.3), kind=kLoop, calls=%fused_computation | loop fusion | bytes 1028 | tf_op jit(solution)/shard_map/dynamic_slice | solution.py:484
  21.1 0.7 %copy.8 = f32[4,8,8,128]{3,2,1,0:T(8,128)} copy(f32[4,8,8,128]{3,2,1,0:T(8,128)S(1)} %get-tuple-element.8) | data formatting | bytes 262144

commit v6 on v5

--- a/solution.py
+++ b/solution.py
@@ -27,7 +27,7 @@
 
 def kernel(
     n_tile, n_store, state_h, cot_h, land_h, count_h, bg_h, out, bg_out,
-    st, ct, land, count, bg,
+    fields_in, cells_in, bg,
     xa, xb, halo_rx, own_rx, dens_tx, dens_rx,
     early, early_rx, ret1, ret1_rx, part, part_rx, back_tx, back_rx,
     in_sem, halo_s, halo_r, own_s, own_r, dens_s, dens_r,
@@ -43,6 +43,13 @@
     owner = jnp.logical_or(s == 0, s == end)
     late = lax.rem(t // 4, 2) == 1
 
+    pltpu.make_async_copy(state_h, fields_in.at[0], in_sem.at[0]).start()
+    pltpu.make_async_copy(cot_h, fields_in.at[1], in_sem.at[0]).start()
+    pltpu.make_async_copy(land_h, cells_in.at[0], in_sem.at[1]).start()
+    pltpu.make_async_copy(count_h, cells_in.at[1], in_sem.at[1]).start()
+    pltpu.make_async_copy(bg_h, bg, in_sem.at[2]).start()
+    st, ct = fields_in.at[0], fields_in.at[1]
+
     barrier = pltpu.get_barrier_semaphore()
 
     def greet(**where):
@@ -58,13 +65,6 @@
     for d in range(2, n_store, 2):
         greet(store=lax.rem(chip + d, n_store))
 
-    loads = [
-        pltpu.make_async_copy(src, dst, in_sem.at[i])
-        for i, (src, dst) in enumerate(((land_h, land), (count_h, count), (bg_h, bg), (state_h, st), (cot_h, ct)))
-    ]
-    for load in loads:
-        load.start()
-
     lane = lax.broadcasted_iota(jnp.int32, (8, 128), 1)
     row = lax.broadcasted_iota(jnp.int32, (8, 128), 0)
     block = lane >> 4
@@ -84,16 +84,21 @@
         copies = []
         for d in range(1, n_store):
             to = lax.rem(s + d, n_store)
-            copies.append(send(src(to), dst.at[s], send_sem.at[d - 1], recv_sem.at[d - 1], {"store": to}))
+            copies.append(send(src(to), dst.at[s], send_sem, recv_sem, {"store": to}))
         return copies
+
+    def arrived(ref, sem):
+        send(ref, ref, sem, sem, {"tile": east}).wait_recv()
+
+    def sent(ref, sem):
+        send(ref, ref, sem, sem, {"tile": east}).wait_send()
+
+    def others(ref):
+        return ref.at[pl.ds(0, n_store - 1)]
 
     def start(copies):
         for copy in copies:
             copy.start()
-
-    def arrived(copies):
-        for copy in copies:
-            copy.wait_recv()
 
     def exchange_blocks(tiles):
         tiles = list(tiles)
@@ -192,9 +197,10 @@
     level = (lax.broadcasted_iota(jnp.int32, (8, 8, 128), 0) + s * 8).astype(F32)
     base = (s * 8).astype(F32)
 
-    for load in loads:
-        load.wait()
-    depth = jnp.where(land[...] == 1, count[...], 0).astype(F32)
+    pltpu.make_async_copy(cells_in, cells_in, in_sem.at[1]).wait()
+    pltpu.make_async_copy(bg, bg, in_sem.at[2]).wait()
+    pltpu.make_async_copy(fields_in, fields_in, in_sem.at[0]).wait()
+    depth = jnp.where(cells_in[0] == 1, cells_in[1], 0).astype(F32)
     wet = jnp.where(level < depth, 1.0, 0.0)
     backgr = bg[...]
     masked = st[...] * wet
@@ -212,7 +218,7 @@
     for side, to in enumerate((east, west)):
         for d in range(n_store):
             far_copies.append(
-                send(xa.at[side], halo_rx.at[side, s], halo_s.at[side, d], halo_r.at[side, s], {"tile": to, "store": d})
+                send(xa.at[side], halo_rx.at[side, s], halo_s, halo_r, {"tile": to, "store": d})
             )
 
     def to_neighbours():
@@ -283,14 +289,14 @@
     early_copies = mates(lambda to: early.at[to], early_rx, early_s, early_r)
     start(early_copies)
     dens_copies = [
-        send(dens_tx.at[0], dens_rx.at[0], dens_s.at[0], dens_r.at[0], {"store": below}),
-        send(dens_tx.at[1], dens_rx.at[1], dens_s.at[1], dens_r.at[1], {"store": above}),
+        send(dens_tx.at[0], dens_rx.at[0], dens_s, dens_r, {"store": below}),
+        send(dens_tx.at[1], dens_rx.at[1], dens_s, dens_r, {"store": above}),
     ]
     start(dens_copies)
     own_copies = mates(lambda to: xb, own_rx, own_s, own_r)
     start(own_copies)
 
-    arrived(early_copies)
+    arrived(others(early_rx), early_r)
     coefs = reduce_blocks([early_rx[j, 2] for j in range(8)])
 
     def four(x):
@@ -311,7 +317,7 @@
     start(ret1_copies)
     pl.when(jnp.logical_not(late))(to_neighbours)
 
-    arrived(dens_copies)
+    arrived(dens_rx, dens_r)
     gate_top = jax.nn.sigmoid(dens_rx[0] - density[0])
     gate_bot = jax.nn.sigmoid(density[7] - dens_rx[1])
     pair_top = jnp.where(base > 0.0, wet[0], 0.0)
@@ -328,7 +334,7 @@
     def finish(p, top, bot):
         return jnp.stack([p[i] + up[i] * top - down[i] * bot for i in range(8)], axis=1)
 
-    arrived(ret1_copies)
+    arrived(others(ret1_rx), ret1_r)
     flux_b = exchange_blocks([ret1_rx[d, 0] for d in range(8)])
     flux_a = exchange_blocks([ret1_rx[d, 1] for d in range(8)])
     top_b, bot_b = jnp.stack(flux_b[:4]), jnp.stack(flux_b[4:])
@@ -346,7 +352,7 @@
     back_tx[...] = beside(pack_edges(jnp.stack([back[f, i] for i in range(8) for f in range(4)]), (32, 16, 8, 2, 1)))
     back_rx[s] = back_tx[...]
     back_copies = [
-        (to, send(back_tx, back_rx.at[s], back_s.at[k], back_r.at[s], {"store": to})) for k, to in enumerate((0, end))
+        (to, send(back_tx, back_rx.at[s], back_s, back_r, {"store": to})) for to in (0, end)
     ]
     for to, copy in back_copies:
         pl.when(s != to)(copy.start)
@@ -362,7 +368,7 @@
     grad_u = grad[2] - ADVECT * jnp.sum(wet_back[:2] * grad_x, axis=0) - latitude * wet_back[3]
     grad_v = grad[3] - ADVECT * jnp.sum(wet_back[:2] * grad_y, axis=0) + latitude * wet_back[2]
 
-    arrived(own_copies)
+    arrived(others(own_rx), own_r)
     own = jnp.stack(exchange_blocks([own_rx[j, 0] for j in range(8)]))
     own_inter = jnp.stack(exchange_blocks([own_rx[j, 1] for j in range(8)]))
     own_dens = edge_density(own)
@@ -374,9 +380,7 @@
     along = jnp.where(field < 2, along, 0.0)
     own_wet = jnp.where(edge_level < own_depth, DIFFUSE, 0.0)
 
-    for side in range(2):
-        for src in range(n_store):
-            send(xa.at[0], halo_rx.at[side, src], halo_s.at[0, 0], halo_r.at[side, src], {"tile": east}).wait_recv()
+    arrived(halo_rx, halo_r)
     halo = jnp.stack(exchange_blocks([sides(halo_rx[1, j], halo_rx[0, j]) for j in range(8)]))
     from_west, from_east = halo_rx[0, 0], halo_rx[1, 0]
     west_depth, east_depth = column(from_west, 0), column(from_east, 1)
@@ -430,14 +434,12 @@
     out[2] = grad_u + edge_flow[2] - pull
     out[3] = grad_v + edge_flow[3]
 
-    arrived(part_copies)
+    arrived(others(part_rx), part_r)
     bg_out[...] = jnp.sum(part_rx[...], axis=0)
 
     @pl.when(owner)
     def _():
-        for d in range(1, n_store):
-            src = lax.rem(s + d, n_store)
-            send(back_tx, back_rx.at[src], back_s.at[0], back_r.at[src], {"store": src}).wait_recv()
+        arrived(others(back_rx), back_r)
         own_back = jnp.stack(exchange_blocks([back_rx[j] for j in range(8)]))
         result = jnp.sum(edge_wet[1:] * (solved[:-1] - solved[1:]) * (own_back[:-1] - own_back[1:]), axis=0)
         jump = (solved[7] - lanes(solved[0], -16)) * (own_back[7] - lanes(own_back[0], -16))
@@ -448,18 +450,25 @@
         result = -(result + lanes(result, -4))
         bg_out[...] = jnp.where(first, result, jnp.where(last, lanes(result, 126), bg_out[...]))
 
-    for to, copy in back_copies:
-        pl.when(s != to)(copy.wait_send)
-    for copies in (far_copies, early_copies, dens_copies, own_copies, ret1_copies, part_copies):
-        for copy in copies:
-            copy.wait_send()
+        sent(back_rx.at[0], back_s)
+
+    @pl.when(jnp.logical_not(owner))
+    def _():
+        sent(back_rx.at[pl.ds(0, 2)], back_s)
+
+    sent(halo_rx, halo_s)
+    sent(dens_rx, dens_s)
+    sent(others(early_rx), early_s)
+    sent(others(own_rx), own_s)
+    sent(others(ret1_rx), ret1_s)
+    sent(others(part_rx), part_s)
 
 
 def shards(n_tile, n_store, state, cotangent, land_mask, wet_count, background):
     tile = (8, 128)
     vmem = functools.partial(pltpu.VMEM, dtype=F32)
     sem = pltpu.SemaphoreType.DMA
-    n, mates = n_store, n_store - 1
+    n = n_store
     grad, bg_sum = pl.pallas_call(
         functools.partial(kernel, n_tile, n_store),
         name="ocean",
@@ -467,17 +476,14 @@
         in_specs=[pl.BlockSpec(memory_space=pltpu.HBM)] * 5,
         out_specs=(pl.BlockSpec(memory_space=pltpu.VMEM), pl.BlockSpec(memory_space=pltpu.VMEM)),
         scratch_shapes=[
-            vmem(state.shape), vmem(state.shape),
-            pltpu.VMEM(tile, jnp.int32), pltpu.VMEM(tile, jnp.int32), vmem(tile),
+            vmem((2,) + state.shape), pltpu.VMEM((2,) + tile, jnp.int32), vmem(tile),
             vmem((2,) + tile), vmem((2,) + tile), vmem((2, n) + tile), vmem((n, 2) + tile),
             vmem((2,) + tile), vmem((2,) + tile),
             vmem((n, 3) + tile), vmem((n, 3) + tile),
             vmem((n, 2) + tile), vmem((n, 2) + tile),
             vmem(tile), vmem((n,) + tile), vmem(tile), vmem((n,) + tile),
-            sem((5,)), sem((2, n)), sem((2, n)), sem((mates,)), sem((mates,)), sem((2,)), sem((2,)),
-            sem((mates,)), sem((mates,)), sem((mates,)), sem((mates,)), sem((mates,)), sem((mates,)),
-            sem((2,)), sem((n,)), pltpu.SemaphoreType.REGULAR, pltpu.SemaphoreType.REGULAR,
-        ],
+            sem((3,)),
+        ] + [sem] * 14 + [pltpu.SemaphoreType.REGULAR] * 2,
         compiler_params=pltpu.CompilerParams(collective_id=0, has_side_effects=True, vmem_limit_bytes=8 << 20),
     )(*[pltpu.with_memory_space_constraint(x, pltpu.HBM) for x in (state, cotangent, land_mask, wet_count, background)])
     part = state.shape[3] // n_store

time: 22 us -> 21.1 us (0.959)
  Pallas kernels: 19.8 us -> 18.8 us
    pallas_call x1, Pallas kernels: 19.8 us -> 18.8 us  [shards(): pl.pallas_call(functools.partial(kernel, n_tile, n_store), name='ocean',...]
where the time goes in v6:
time: 21.1 us; the launch traced here: 20.8 us
  Pallas kernels  18.8 us (89%)
  local copies, waits for them, and re-layouts  1.33 us (6%)
  between operations  0.64 us (3%)
    pallas_call x1, Pallas kernels, shards(): pl.pallas_call(functools.partial(kernel, n_tile, n_store), name='ocean',...  18.8 us
    dynamic_slice x1, local copies, waits for them, and re-layouts, shards(): lax.dynamic_slice_in_dim(bg_sum, lax.axis_index('store') * part, part, 1)  0.67 us
    unnamed x1, local copies, waits for them, and re-layouts  0.65 us

profile of v6, /device:TPU:1, one launch (start us, length us, event | category | flops | bytes accessed | tf_op | source)
XLA Modules:
  0.0 20.8 jit_solution(9643047147408286182)
XLA Ops:
  0.6 18.8 %ocean.1 = (f32[4,8,8,128]{3,2,1,0:T(8,128)S(1)}, f32[8,128]{1,0:T(8,128)S(1)}) custom-call(f32[4,8,8,128]{3,2,1,0:T(8,128)} %state_h.1, f32[4,8,8,128]{3,2,1,0:T(8,128)} %cot_h.1, s32[8,128]{1,0:T(8,128)} %land_h.1, s32[8,128]{1,0:T(8,128)} %count_h.1, f32[8,128]{1,0:T(8,128)} %bg_h.1), custom_call_target="tpu_custom_call" | custom-call | tf_op jit(solution)/shard_map/ocean/pallas_call | solution.py:472
  19.5 0.7 %constant_dynamic-slice_fusion = f32[8,16]{1,0:T(8,128)} fusion(f32[8,128]{1,0:T(8,128)S(1)} %get-tuple-element.5, s32[]{:T(128)S(6)} %select_n.3), kind=kLoop, calls=%fused_computation | loop fusion | bytes 1028 | tf_op jit(solution)/shard_map/dynamic_slice | solution.py:490
  20.1 0.7 %copy.8 = f32[4,8,8,128]{3,2,1,0:T(8,128)} copy(f32[4,8,8,128]{3,2,1,0:T(8,128)S(1)} %get-tuple-element.8) | data formatting | bytes 262144

commit v7 on v6

--- a/solution.py
+++ b/solution.py
@@ -28,9 +28,9 @@
 def kernel(
     n_tile, n_store, state_h, cot_h, land_h, count_h, bg_h, out, bg_out,
     fields_in, cells_in, bg,
-    xa, xb, halo_rx, own_rx, dens_tx, dens_rx,
+    xa, ya, xb, halo_rx, side_rx, own_rx, dens_tx, dens_rx,
     early, early_rx, ret1, ret1_rx, part, part_rx, back_tx, back_rx,
-    in_sem, halo_s, halo_r, own_s, own_r, dens_s, dens_r,
+    in_sem, halo_s, halo_r, side_s, side_r, own_s, own_r, dens_s, dens_r,
     early_s, early_r, ret1_s, ret1_r, part_s, part_r, back_s, back_r, near, far,
 ):
     t = lax.axis_index("tile")
@@ -132,31 +132,49 @@
         return jnp.where(row == 0, 0.0, rows(x, 1))
 
     def eliminate(mix):
-        ratio, inverse = [], []
-        excess = jnp.ones((8, 128), F32)
-        for i in range(7):
-            inv = 1.0 / (excess + mix[i])
-            ratio.append(mix[i] * inv)
-            inverse.append(inv)
-            excess = 1.0 + ratio[i] * excess
-        inverse.append(1.0 / excess)
-        up = [inverse[0]]
-        for i in range(1, 8):
-            up.append(mix[i - 1] * up[-1] * inverse[i])
-        for i in range(6, -1, -1):
+        ratio, inverse = [None] * 8, [None] * 8
+        above_excess = jnp.ones((8, 128), F32)
+        below_excess = jnp.ones((8, 128), F32)
+        for i in range(4):
+            inverse[i] = 1.0 / (above_excess + mix[i])
+            ratio[i] = mix[i] * inverse[i]
+            above_excess = 1.0 + ratio[i] * above_excess
+        for i in (7, 6, 5):
+            inverse[i] = 1.0 / (below_excess + mix[i - 1])
+            ratio[i] = mix[i - 1] * inverse[i]
+            below_excess = 1.0 + ratio[i] * below_excess
+        inverse[4] = 1.0 / (above_excess + (below_excess - 1.0))
+        up, down = [None] * 8, [None] * 8
+        up[0] = inverse[0]
+        for i in range(1, 5):
+            up[i] = mix[i - 1] * up[i - 1] * inverse[i]
+        for i in (3, 2, 1, 0):
             up[i] = up[i] + ratio[i] * up[i + 1]
-        down = [None] * 7 + [inverse[7]]
-        for i in range(6, -1, -1):
+        for i in (5, 6, 7):
+            up[i] = ratio[i] * up[i - 1]
+        down[7] = inverse[7]
+        for i in (6, 5, 4):
+            down[i] = mix[i] * down[i + 1] * inverse[i]
+        for i in (3, 2, 1, 0):
             down[i] = ratio[i] * down[i + 1]
+        for i in (5, 6, 7):
+            down[i] = down[i] + ratio[i] * down[i - 1]
         return (mix, ratio, inverse), up, down
 
     def local_solve(system, rhs):
         mix, ratio, inverse = system
-        values = [rhs[0] * inverse[0]]
-        for i in range(1, 8):
-            values.append((rhs[i] + mix[i - 1] * values[-1]) * inverse[i])
-        for i in range(6, -1, -1):
+        values = [None] * 8
+        values[0] = rhs[0] * inverse[0]
+        for i in range(1, 4):
+            values[i] = (rhs[i] + mix[i - 1] * values[i - 1]) * inverse[i]
+        values[7] = rhs[7] * inverse[7]
+        for i in (6, 5):
+            values[i] = (rhs[i] + mix[i] * values[i + 1]) * inverse[i]
+        values[4] = (rhs[4] + mix[3] * values[3] + mix[4] * values[5]) * inverse[4]
+        for i in (3, 2, 1, 0):
             values[i] = values[i] + ratio[i] * values[i + 1]
+        for i in (5, 6, 7):
+            values[i] = values[i] + ratio[i] * values[i - 1]
         return values
 
     def edge_density(tiles):
@@ -169,29 +187,38 @@
         return jnp.where(even, a, b)
 
     def reduce_blocks(tiles):
-        m_inv, low, high = [], [], []
+        rows_m, diag, lower, upper = [], [], [], []
         for j in range(7):
             here, there = tiles[j], tiles[j + 1]
             weight = lanes(here, -80)
             gates = jax.nn.sigmoid(lanes(here, -64) - lanes(there, -48))
             m = jnp.where(weight > 0.0, weight + MIXING * gates, 0.0)
-            pivot = 1.0 + m * (lanes(here, -32) + there)
-            lower = m * lanes(here, -16)
-            if j:
-                pivot = pivot - lower * high[-1]
-            inv = 1.0 / jnp.where(block == 0, pivot, 1.0)
-            m_inv.append(m * inv)
-            low.append(lower * inv)
-            high.append(m * lanes(there, -16) * inv)
-        return m_inv, low, high
+            rows_m.append(m)
+            diag.append(1.0 + m * (lanes(here, -32) + there))
+            lower.append(m * lanes(here, -16))
+            upper.append(m * lanes(there, -16))
+        inv = [None] * 7
+
+        def invert(j, pivot):
+            inv[j] = 1.0 / jnp.where(block == 0, pivot, 1.0)
+
+        invert(0, diag[0])
+        invert(6, diag[6])
+        for j, k in ((1, 5), (2, 4)):
+            invert(j, diag[j] - lower[j] * (upper[j - 1] * inv[j - 1]))
+            invert(k, diag[k] - upper[k] * (lower[k + 1] * inv[k + 1]))
+        invert(3, diag[3] - lower[3] * (upper[2] * inv[2]) - upper[3] * (lower[4] * inv[4]))
+        return tuple([x[j] * inv[j] for j in range(7)] for x in (rows_m, lower, upper))
 
     def fluxes(m_inv, low, high, jumps):
-        flux = []
-        for j in range(7):
-            value = m_inv[j] * jumps[j]
-            flux.append(value + low[j] * flux[-1] if j else value)
-        for j in range(5, -1, -1):
+        flux = [m_inv[j] * jumps[j] for j in range(7)]
+        for j, k in ((1, 5), (2, 4)):
+            flux[j] = flux[j] + low[j] * flux[j - 1]
+            flux[k] = flux[k] + high[k] * flux[k + 1]
+        flux[3] = flux[3] + low[3] * flux[2] + high[3] * flux[4]
+        for j, k in ((2, 4), (1, 5), (0, 6)):
             flux[j] = flux[j] + high[j] * flux[j + 1]
+            flux[k] = flux[k] + low[k] * flux[k - 1]
         return flux
 
     level = (lax.broadcasted_iota(jnp.int32, (8, 8, 128), 0) + s * 8).astype(F32)
@@ -205,21 +232,26 @@
     backgr = bg[...]
     masked = st[...] * wet
     fields = [masked[f] for f in range(4)] + [ct[f] for f in range(4)]
-    packed = pack_edges(jnp.stack([fields[f][i] for i in range(8) for f in range(8)]), (32, 16, 8, 4, 2, 1))
-    own_edges = beside(packed)
-
-    def extra(c):
-        return jnp.where(field == 0, column(depth, c), column(backgr, c))
-
-    xa[0] = sides(extra(127), own_edges)
-    xa[1] = sides(own_edges, extra(0))
-    xb[0] = own_edges
+    def store_edges():
+        packed = pack_edges(jnp.stack([fields[f][i] for i in range(8) for f in range(8)]), (32, 16, 8, 4, 2, 1))
+        own_edges = beside(packed)
+
+        turned = rows(own_edges, 4)
+        xa[0] = sides(lanes(own_edges, -1), turned)
+        xa[1] = sides(own_edges, lanes(turned, 1))
+        ya[...] = jnp.where(jnp.logical_or(lane < 32, lane >= 96), depth, lanes(backgr, 64))
+        xb[0] = own_edges
+    pl.when(late)(store_edges)
+
     far_copies = []
     for side, to in enumerate((east, west)):
         for d in range(n_store):
+            half = pl.ds(4 - 4 * side, 4)
             far_copies.append(
-                send(xa.at[side], halo_rx.at[side, s], halo_s, halo_r, {"tile": to, "store": d})
+                send(xa.at[side, pl.ds(0, 4)], halo_rx.at[s, half], halo_s, halo_r, {"tile": to, "store": d})
             )
+    far_copies.append(send(ya, side_rx.at[0], side_s, side_r, {"tile": east}))
+    far_copies.append(send(ya, side_rx.at[1], side_s, side_r, {"tile": west}))
 
     def to_neighbours():
         @pl.when(core == 1)
@@ -260,7 +292,7 @@
     grad_y = m_north[:2] - m_south[:2]
     advect = -ADVECT * (zonal * grad_x + merid * grad_y)
     inter = [inter[0] + advect[0], inter[1] + advect[1], inter[2] + latitude * merid, inter[3] - latitude * zonal]
-    xb[1] = beside(pack_edges(jnp.stack([inter[f][i] for i in range(8) for f in range(4)]), (32, 16, 8, 2, 1)))
+    inter_edges = [inter[f][i] for i in range(8) for f in range(4)]
     inter = jnp.stack(inter)
     p_after = local_solve(system, [inter[:, i] for i in range(8)])
 
@@ -275,7 +307,6 @@
         for d, tile in enumerate(exchange_blocks(group)):
             early[d, g] = tile
     early_rx[s] = early[s]
-    own_rx[s] = xb[...]
 
     @pl.when(core == 0)
     def _():
@@ -293,6 +324,9 @@
         send(dens_tx.at[1], dens_rx.at[1], dens_s, dens_r, {"store": above}),
     ]
     start(dens_copies)
+    pl.when(jnp.logical_not(late))(store_edges)
+    xb[1] = beside(pack_edges(jnp.stack(inter_edges), (32, 16, 8, 2, 1)))
+    own_rx[s] = xb[...]
     own_copies = mates(lambda to: xb, own_rx, own_s, own_r)
     start(own_copies)
 
@@ -381,13 +415,19 @@
     own_wet = jnp.where(edge_level < own_depth, DIFFUSE, 0.0)
 
     arrived(halo_rx, halo_r)
-    halo = jnp.stack(exchange_blocks([sides(halo_rx[1, j], halo_rx[0, j]) for j in range(8)]))
-    from_west, from_east = halo_rx[0, 0], halo_rx[1, 0]
-    west_depth, east_depth = column(from_west, 0), column(from_east, 1)
+    arrived(side_rx, side_r)
+
+    def unmix(x):
+        turned = rows(x, 4)
+        return jnp.where(even == (row < 4), x, sides(lanes(turned, -1), lanes(turned, 1)))
+
+    halo = unmix(jnp.stack(exchange_blocks([halo_rx[j] for j in range(8)])))
+    from_west, from_east = side_rx[0], side_rx[1]
+    west_depth, east_depth = column(from_west, 127), column(from_east, 0)
     inner = field < 4
     dens = jnp.where(inner, own_dens, edge_density(halo))
     depths = jnp.where(inner, own_depth, sides(east_depth, west_depth))
-    backs = jnp.where(inner, own_bg, sides(column(from_east, 3), column(from_west, 2)))
+    backs = jnp.where(inner, own_bg, sides(column(from_east, 64), column(from_west, 63)))
     edge_wet = jnp.where(edge_level < depths, 1.0, 0.0)
     halo_wet = jnp.where(edge_level < sides(west_depth, east_depth), 1.0, 0.0)
     swapped = sides(lanes(halo, -1), lanes(halo, 1))
@@ -414,7 +454,7 @@
     top_a = jnp.where(edge, own_here[:, 8], top_a)
     bot_a = jnp.where(edge, own_here[:, 9], bot_a)
     b_edge = jnp.stack([lanes(here[:8], 119 - 2 * f) for f in range(4)])
-    cols = sides(halo_rx[1, s], halo_rx[0, s])
+    cols = unmix(halo_rx[s])
     cols = jnp.stack([lanes(cols, -16 * i) for i in range(8)])
     m_edge = jnp.stack([lanes(cols, 127 - 2 * f) for f in range(3)])
     beside_wet = jnp.where(jnp.logical_and(edge, level < jnp.where(last, east_depth, west_depth)), DIFFUSE * wet, 0.0)
@@ -457,6 +497,7 @@
         sent(back_rx.at[pl.ds(0, 2)], back_s)
 
     sent(halo_rx, halo_s)
+    sent(side_rx, side_s)
     sent(dens_rx, dens_s)
     sent(others(early_rx), early_s)
     sent(others(own_rx), own_s)
@@ -477,13 +518,13 @@
         out_specs=(pl.BlockSpec(memory_space=pltpu.VMEM), pl.BlockSpec(memory_space=pltpu.VMEM)),
         scratch_shapes=[
             vmem((2,) + state.shape), pltpu.VMEM((2,) + tile, jnp.int32), vmem(tile),
-            vmem((2,) + tile), vmem((2,) + tile), vmem((2, n) + tile), vmem((n, 2) + tile),
+            vmem((2,) + tile), vmem(tile), vmem((2,) + tile), vmem((n,) + tile), vmem((2,) + tile), vmem((n, 2) + tile),
             vmem((2,) + tile), vmem((2,) + tile),
             vmem((n, 3) + tile), vmem((n, 3) + tile),
             vmem((n, 2) + tile), vmem((n, 2) + tile),
             vmem(tile), vmem((n,) + tile), vmem(tile), vmem((n,) + tile),
             sem((3,)),
-        ] + [sem] * 14 + [pltpu.SemaphoreType.REGULAR] * 2,
+        ] + [sem] * 16 + [pltpu.SemaphoreType.REGULAR] * 2,
         compiler_params=pltpu.CompilerParams(collective_id=0, has_side_effects=True, vmem_limit_bytes=8 << 20),
     )(*[pltpu.with_memory_space_constraint(x, pltpu.HBM) for x in (state, cotangent, land_mask, wet_count, background)])
     part = state.shape[3] // n_store

time: 21.1 us -> 20.8 us (0.986); the launches traced: 20.8 us -> 20.7 us
  no operation moved by 1% of the time
where the time goes in v7:
time: 20.8 us; the launch traced here: 20.7 us
  Pallas kernels  18.8 us (90%)
  local copies, waits for them, and re-layouts  1.33 us (6%)
  between operations  0.64 us (3%)
    pallas_call x1, Pallas kernels, shards(): pl.pallas_call(functools.partial(kernel, n_tile, n_store), name='ocean',...  18.8 us
    dynamic_slice x1, local copies, waits for them, and re-layouts, shards(): lax.dynamic_slice_in_dim(bg_sum, lax.axis_index('store') * part, part, 1)  0.67 us
    unnamed x1, local copies, waits for them, and re-layouts  0.65 us

profile of v7, /device:TPU:1, one launch (start us, length us, event | category | flops | bytes accessed | tf_op | source)
XLA Modules:
  0.0 20.7 jit_solution(3213101164244400348)
XLA Ops:
  0.6 18.8 %ocean.1 = (f32[4,8,8,128]{3,2,1,0:T(8,128)S(1)}, f32[8,128]{1,0:T(8,128)S(1)}) custom-call(f32[4,8,8,128]{3,2,1,0:T(8,128)} %state_h.1, f32[4,8,8,128]{3,2,1,0:T(8,128)} %cot_h.1, s32[8,128]{1,0:T(8,128)} %land_h.1, s32[8,128]{1,0:T(8,128)} %count_h.1, f32[8,128]{1,0:T(8,128)} %bg_h.1), custom_call_target="tpu_custom_call" | custom-call | tf_op jit(solution)/shard_map/ocean/pallas_call | solution.py:513
  19.4 0.7 %constant_dynamic-slice_fusion = f32[8,16]{1,0:T(8,128)} fusion(f32[8,128]{1,0:T(8,128)S(1)} %get-tuple-element.5, s32[]{:T(128)S(6)} %select_n.3), kind=kLoop, calls=%fused_computation | loop fusion | bytes 1028 | tf_op jit(solution)/shard_map/dynamic_slice | solution.py:531
  20.1 0.7 %copy.8 = f32[4,8,8,128]{3,2,1,0:T(8,128)} copy(f32[4,8,8,128]{3,2,1,0:T(8,128)S(1)} %get-tuple-element.8) | data formatting | bytes 262144

commit v8 on v7

--- a/solution.py
+++ b/solution.py
@@ -475,7 +475,10 @@
     out[3] = grad_v + edge_flow[3]
 
     arrived(others(part_rx), part_r)
-    bg_out[...] = jnp.sum(part_rx[...], axis=0)
+    total = jnp.sum(part_rx[...], axis=0)
+    for bit in (1, 2, 4):
+        total = jnp.where((s & bit) != 0, lanes(total, -16 * bit), total)
+    bg_out[...] = total
 
     @pl.when(owner)
     def _():
@@ -488,7 +491,9 @@
             result = result + lanes(result, shift)
         result = result + lanes(result, -2)
         result = -(result + lanes(result, -4))
-        bg_out[...] = jnp.where(first, result, jnp.where(last, lanes(result, 126), bg_out[...]))
+        at_west = jnp.logical_and(first, s == 0)
+        at_east = jnp.logical_and(lane == 15, s == end)
+        bg_out[...] = jnp.where(at_west, result, jnp.where(at_east, lanes(result, 14), bg_out[...]))
 
         sent(back_rx.at[0], back_s)
 
@@ -503,6 +508,16 @@
     sent(others(own_rx), own_s)
     sent(others(ret1_rx), ret1_s)
     sent(others(part_rx), part_s)
+
+
+def write_out(grad, bg_sum, out, bg_out, held, out_sem, bg_sem):
+    copy = pltpu.make_async_copy(grad, out, out_sem)
+    copy.start()
+    held[...] = bg_sum[:, :16]
+    bg_copy = pltpu.make_async_copy(held, bg_out, bg_sem)
+    bg_copy.start()
+    copy.wait()
+    bg_copy.wait()
 
 
 def shards(n_tile, n_store, state, cotangent, land_mask, wet_count, background):
@@ -527,8 +542,16 @@
         ] + [sem] * 16 + [pltpu.SemaphoreType.REGULAR] * 2,
         compiler_params=pltpu.CompilerParams(collective_id=0, has_side_effects=True, vmem_limit_bytes=8 << 20),
     )(*[pltpu.with_memory_space_constraint(x, pltpu.HBM) for x in (state, cotangent, land_mask, wet_count, background)])
-    part = state.shape[3] // n_store
-    return grad, lax.dynamic_slice_in_dim(bg_sum, lax.axis_index("store") * part, part, 1)
+    columns = jax.ShapeDtypeStruct((8, state.shape[3] // n_store), F32)
+    return pl.pallas_call(
+        write_out,
+        name="write_out",
+        out_shape=(jax.ShapeDtypeStruct(state.shape, F32), columns),
+        in_specs=[pl.BlockSpec(memory_space=pltpu.VMEM)] * 2,
+        out_specs=(pl.BlockSpec(memory_space=pl.ANY), pl.BlockSpec(memory_space=pl.ANY)),
+        scratch_shapes=[vmem(columns.shape), sem, sem],
+        compiler_params=pltpu.CompilerParams(vmem_limit_bytes=8 << 20),
+    )(grad, bg_sum)
 
 
 def solution(mesh):

time: 20.8 us -> 20.4 us (0.981)
  local copies, waits for them, and re-layouts: 1.33 us -> 0 us
  Pallas kernels: 18.8 us -> 19.6 us
    pallas_call x0 -> x1, Pallas kernels: none -> 0.68 us  [shards(): pl.pallas_call(write_out, name='write_out', out_shape=(jax.ShapeDtypeStru...]
    dynamic_slice x1 -> x0, local copies, waits for them, and re-layouts: 0.67 us -> none  [shards(): lax.dynamic_slice_in_dim(bg_sum, lax.axis_index('store') * part, part, 1)]
    unnamed x1 -> x0, local copies, waits for them, and re-layouts: 0.65 us -> none
where the time goes in v8:
time: 20.4 us; the launch traced here: 20.3 us
  Pallas kernels  19.6 us (96%)
  between operations  0.64 us (3%)
    pallas_call x1, Pallas kernels, shards(): pl.pallas_call(functools.partial(kernel, n_tile, n_store), name='ocean',...  19 us
    pallas_call x1, Pallas kernels, shards(): pl.pallas_call(write_out, name='write_out', out_shape=(jax.ShapeDtypeStru...  0.68 us

profile of v8, /device:TPU:1, one launch (start us, length us, event | category | flops | bytes accessed | tf_op | source)
XLA Modules:
  0.0 20.3 jit_solution(8478999172533347993)
XLA Ops:
  0.6 19.0 %ocean.1 = (f32[4,8,8,128]{3,2,1,0:T(8,128)S(1)}, f32[8,128]{1,0:T(8,128)S(1)}) custom-call(f32[4,8,8,128]{3,2,1,0:T(8,128)} %state_h.1, f32[4,8,8,128]{3,2,1,0:T(8,128)} %cot_h.1, s32[8,128]{1,0:T(8,128)} %land_h.1, s32[8,128]{1,0:T(8,128)} %count_h.1, f32[8,128]{1,0:T(8,128)} %bg_h.1), custom_call_target="tpu_custom_call" | custom-call | tf_op jit(solution)/shard_map/ocean/pallas_call | solution.py:528
  19.6 0.7 %write_out.1 = (f32[4,8,8,128]{3,2,1,0:T(8,128)}, f32[8,16]{1,0:T(8,128)}) custom-call(f32[4,8,8,128]{3,2,1,0:T(8,128)S(1)} %get-tuple-element.4.grad, f32[8,128]{1,0:T(8,128)S(1)} %get-tuple-element.5.bg_sum), custom_call_target="tpu_custom_call" | custom-call | tf_op jit(solution)/shard_map/write_out/pallas_call | solution.py:546
